TPU v7x, 32 devices: a whole 2x2x4 slice. The times are simulated.
32 devices in a mesh: lon: 16 (over z, x, core), lat: 2 (over y).
Axes of the slice: x: 2, y: 2, z: 4, core: 2. Of those that a mesh axis runs over, the one named last changes fastest.
Arguments:
- spec_pts: bfloat16 [36, 36, 16384], P(None, None, ('lon', 'lat')), may hold values from 0.049804688 to 2
- wind_u: float32 [16384], P(('lon', 'lat')), may hold values from -40 to 40
- wind_v: float32 [16384], P(('lon', 'lat')), may hold values from -40 to 40
- ocean_current: bfloat16 [2, 2, 128, 128], P(None, 'lat', 'lon'), may hold values from -0.099609375 to 0.099609375
- block_owner: int32 [8, 16], P('lat', 'lon'), may hold values from 0 to 15, as said below
- block_slot: int32 [8, 16], P('lat', 'lon'), may hold values from 0 to 7, as said below
- cell_source: int32 [8, 2048], P('lat', 'lon'), may hold values from 0 to 511, as said below
- land_mask: int32 [8, 2048], P('lat', 'lon'), may hold values 0 or 1
Outputs:
- spectrum_out: bfloat16 [36, 36, 8, 2048], P(None, None, 'lat', 'lon')
Inputs may be any that keep to these rules, and one draw needn't show every extreme that they name: Within each band of 4 grid rows, the pairs (block_owner, block_slot) over all its rows and tile columns are distinct, each owner's slots run from 0 to its count of blocks minus one; an owner holds between 0 and 8 blocks, and at least one owner holds exactly 8. `block_slot`: see block_owner. `cell_source`: within each tile of 4 x 128 cells, the values are a permutation of 0 to 511.
All inputs are finite; a program needn't handle non-finite values. No bound on the sum of `land_mask` on one device may be relied on, other than what follows from the above.
Results may differ from a plain program's by a relative error of at most 0.001.
The roundings to bfloat16 on the way count: a program that leaves them out, or rounds other values in their place, can miss the bound.
Values may be sent and summed in bfloat16 or wider, within the bound.
No kernel may reach another device: no remote copies, remote signals or barrier semaphores. Data moves between devices by JAX's collectives and lax.ppermute only.
A program may use at most 128 MiB of HBM per device.

v0:
```python
import jax
import jax.numpy as jnp
from jax import lax
from jax.sharding import PartitionSpec as P

fastest = 0.53
turn_scale = 2.5


def with_halo(shard, sides, width, wrap):
    for axis, dim in sides:
        devices, length = (lax.axis_size(axis), shard.shape[dim])
        up = [(i, (i + 1) % devices) for i in range(devices if wrap else devices - 1)]
        down = [(j, i) for i, j in up]
        last = lax.slice_in_dim(shard, length - width, length, axis=dim)
        leading = lax.slice_in_dim(shard, 0, width, axis=dim)
        before = lax.ppermute(last, axis, up)
        after = lax.ppermute(leading, axis, down)
        shard = jnp.concatenate([before, shard, after], axis=dim)
    return shard


def tables(freqs, dirs):
    ratio = 1.1 ** jnp.arange(freqs).astype(jnp.float32)
    group_speed = fastest / ratio
    phase_speed = 44.6 / ratio
    relative = ratio / ratio[freqs - 1]
    spacing = 2.0 * jnp.pi / dirs
    theta = (jnp.arange(dirs).astype(jnp.float32) + 0.5) * spacing
    facing = (jnp.arange(dirs).astype(jnp.float32) + 1.0) * spacing
    return (
        group_speed,
        phase_speed,
        relative,
        jnp.cos(theta),
        jnp.sin(theta),
        jnp.cos(facing),
        jnp.sin(facing),
    )


def grow(energy, proj, phase_val, rel_val, mean_energy):
    drive = jnp.maximum(proj / phase_val - 1.0, 0.0)
    gain = 0.5 * jnp.tanh(0.2 * drive)
    loss = 0.3 * rel_val * (mean_energy / 0.5) ** 2
    return (energy * jnp.exp(gain - loss)).astype(jnp.bfloat16)


def turning(ux, uy, vx, vy, face_cos, face_sin):
    return turn_scale * (
        face_sin * face_cos * (ux - vy) + face_sin * face_sin * uy - face_cos * face_cos * vx
    )


def body(spec_pts, wind_u, wind_v, ocean_current, block_owner, block_slot, cell_source, land_mask):
    freqs, dirs, points = spec_pts.shape
    lat_rows, lon_cells = cell_source.shape
    n_lon = lax.axis_size("lon")
    n_lat = lax.axis_size("lat")
    per_dest = points // (n_lon * n_lat)
    capacity = ocean_current.shape[2]
    spectral = freqs * dirs
    group_speed, phase_speed, relative, cosd, sind, face_cos, face_sin = tables(freqs, dirs)
    wanted = block_owner[:, 0] * capacity + block_slot[:, 0]
    piece = lax.all_gather(ocean_current, "lon", axis=2, tiled=True)
    count = piece.shape[2]
    inside = (wanted >= 0) & (wanted < count)
    taken = jnp.take(piece[:, 0], jnp.clip(wanted, 0, count - 1), axis=1)
    currents = jnp.where(
        inside[None, :, None], taken, jnp.zeros((2, lat_rows, lon_cells), jnp.bfloat16)
    )
    mean_energy = jnp.sum(spec_pts.astype(jnp.float32), axis=(0, 1)) / (freqs * dirs)
    proj = wind_u[None, :] * cosd[:, None] + wind_v[None, :] * sind[:, None]
    sourced = grow(
        spec_pts.astype(jnp.float32),
        proj[None],
        phase_speed[:, None, None],
        relative[:, None, None],
        mean_energy[None, None, :],
    )
    packed = sourced.reshape(spectral, points).T.reshape(n_lat, n_lon, per_dest, spectral)
    section = lax.all_to_all(packed, "lat", split_axis=0, concat_axis=0, tiled=True)
    moved_in = lax.all_to_all(section, "lon", split_axis=1, concat_axis=1, tiled=True)
    regrouped = moved_in.reshape(points, spectral)
    sea_bf = land_mask.astype(jnp.bfloat16)
    picked = jnp.take(regrouped, cell_source.reshape(-1), axis=0).reshape(
        lat_rows, lon_cells, spectral
    )
    tile = picked.transpose(0, 2, 1) * sea_bf[:, None, :]
    extras = jnp.stack([currents[0], currents[1], sea_bf], axis=1)
    wide_tile, wide_extra = (
        with_halo(tile, (("lon", 2),), 1, True),
        with_halo(extras, (("lon", 2),), 1, True),
    )
    tall_tile, tall_extra = (
        with_halo(tile, (("lat", 0),), 1, False),
        with_halo(extras, (("lat", 0),), 1, False),
    )
    energy = tile.astype(jnp.float32).reshape(lat_rows, freqs, dirs, lon_cells)
    wide = wide_tile.astype(jnp.float32).reshape(lat_rows, freqs, dirs, lon_cells + 2)
    tall = tall_tile.astype(jnp.float32).reshape(lat_rows + 2, freqs, dirs, lon_cells)
    wide_aux = wide_extra.astype(jnp.float32)
    tall_aux = tall_extra.astype(jnp.float32)
    speed_grid = group_speed[None, :, None, None]
    wide_u, wide_v, wide_sea = (wide_aux[:, 0], wide_aux[:, 1], wide_aux[:, 2])
    open_x = wide_sea[:, :-1] * wide_sea[:, 1:]
    face_u = 0.5 * (wide_u[:, :-1] + wide_u[:, 1:])
    cx = speed_grid * cosd[None, None, :, None] + face_u[:, None, None, :]
    flux_x = open_x[:, None, None, :] * (
        jnp.maximum(cx, 0.0) * wide[..., :-1] + jnp.minimum(cx, 0.0) * wide[..., 1:]
    )
    div_x = flux_x[..., 1:] - flux_x[..., :-1]
    tall_u, tall_v, tall_sea = (tall_aux[:, 0], tall_aux[:, 1], tall_aux[:, 2])
    open_y = tall_sea[:-1] * tall_sea[1:]
    face_v = 0.5 * (tall_v[:-1] + tall_v[1:])
    cy = speed_grid * sind[None, None, :, None] + face_v[:, None, None, :]
    flux_y = open_y[:, None, None, :] * (
        jnp.maximum(cy, 0.0) * tall[:-1] + jnp.minimum(cy, 0.0) * tall[1:]
    )
    div_y = flux_y[1:] - flux_y[:-1]
    moved = energy - div_x - div_y
    ux = 0.5 * (wide_u[:, 2:] - wide_u[:, :-2])
    vx = 0.5 * (wide_v[:, 2:] - wide_v[:, :-2])
    uy = 0.5 * (tall_u[2:] - tall_u[:-2])
    vy = 0.5 * (tall_v[2:] - tall_v[:-2])
    turn = turning(
        ux[:, None, :],
        uy[:, None, :],
        vx[:, None, :],
        vy[:, None, :],
        face_cos[None, :, None],
        face_sin[None, :, None],
    )
    turn_grid = turn[:, None]
    upper = jnp.roll(moved, -1, axis=2)
    flux_turn = jnp.maximum(turn_grid, 0.0) * moved + jnp.minimum(turn_grid, 0.0) * upper
    turned = moved - (flux_turn - jnp.roll(flux_turn, 1, axis=2))
    sea = land_mask.astype(jnp.float32)
    result = (turned * sea[:, None, None, :]).astype(jnp.bfloat16)
    return result.transpose(1, 2, 0, 3)


def solution(mesh):
    return jax.shard_map(
        body,
        mesh=mesh,
        in_specs=(
            P(None, None, ("lon", "lat")),
            P(("lon", "lat")),
            P(("lon", "lat")),
            P(None, "lat", "lon", None),
            P("lat", "lon"),
            P("lat", "lon"),
            P("lat", "lon"),
            P("lat", "lon"),
        ),
        out_specs=P(None, None, "lat", "lon"),
        check_vma=False,
    )
```

profile of v0, /device:TPU:0, one launch (start us, length us, event | category | flops | bytes accessed | tf_op | source)
XLA Modules:
  0.0 162.0 jit_solution(6554661810696122520)
XLA Ops:
  0.1 1.7 %convert_reduce_fusion = f32[512]{0:T(512)S(1)} fusion(bf16[36,36,512]{2,1,0:T(8,128)(2,1)} %param.8), kind=kLoop, calls=%fused_computation.15 | loop fusion | flops 1326592 | bytes 1329152 | tf_op jit(solution)/shard_map/reduce_sum | solution.py:72
  1.8 0.6 slice.155
  2.3 0.7 divide_multiply_fusion
  3.1 0.8 multiply_add_fusion
  3.9 2.6 %fusion.14 = bf16[36,36,512]{2,1,0:T(8,128)(2,1)S(1)} fusion(bf16[36,36,512]{2,1,0:T(8,128)(2,1)} %param.8, f32[36,512]{1,0:T(8,128)S(1)} %broadcast_multiply_fusion, f32[36]{0:T(128)S(1)} %fusion.41, f32[36,512]{1,0:T(8,128)S(1)} %multiply_add_fusion), kind=kLoop, calls=%fused_computation.23 | loop fusion | flops 5971968 | bytes 2801808 | tf_op jit(solution)/shard_map/convert_element_type | solution.py:46
  6.5 0.3 reshape.362
  6.8 1.6 copy.76
  8.4 4.3 %all-to-all-start = ((bf16[2,16,16,1296]{3,2,1,0:T(8,128)(2,1)}), bf16[2,16,16,1296]{3,2,1,0:T(8,128)(2,1)S(1)}, u32[]{:S(2)}, u32[]{:S(2)}) async-start(bf16[2,16,16,1296]{3,2,1,0:T(8,128)(2,1)} %bitcast.2), calls=%async_computation | async-start | bytes 2883584 | tf_op jit(solution)/shard_map/all_to_all | solution.py:82
  12.7 22.7 %all_gather.3 = bf16[2,1,128,128]{3,0,1,2:T(2,128)(2,1)S(1)} all-gather(bf16[2,1,8,128]{3,0,1,2:T(2,128)(2,1)S(1)} %copy.82), channel_id=1, replica_groups=mesh['lon'=16,'lat'=2] {'lon'}, dimensions={2}, use_global_device_ids=true | all-gather | bytes 69632 | tf_op jit(solution)/shard_map/all_gather | solution.py:65
  35.4 0.6 gather_fusion.1
  36.1 1.3 collective-permute-start.5
  37.4 4.5 %collective-permute-start.4 = (bf16[1,3,128]{2,0,1:T(2,128)(2,1)S(1)}, bf16[1,3,128]{2,0,1:T(2,128)(2,1)S(1)}, u32[]{:S(2)}, u32[]{:S(2)}) collective-permute-start(bf16[1,3,128]{2,0,1:T(2,128)(2,1)S(1)} %get-tuple-element.22), channel_id=1, source_target_pairs={{0,1},{2,3},{4,5},{6,7},{8,9},{10,11},{12,13},{14,15},{16,17},{18,... | collective-permute-start | bytes 2312 | tf_op jit(solution)/shard_map/ppermute | solution.py:17
  42.1 0.5 collective-permute-start
  42.6 1.3 copy.77
  43.9 5.4 %all-to-all-start.1 = ((bf16[2,16,16,1296]{3,2,0,1:T(8,128)(2,1)}), bf16[2,16,16,1296]{3,2,0,1:T(8,128)(2,1)S(1)}, u32[]{:S(2)}, u32[]{:S(2)}) async-start(bf16[2,16,16,1296]{3,2,0,1:T(8,128)(2,1)} %copy.77), calls=%async_computation.1 | async-start | bytes 2883584 | tf_op jit(solution)/shard_map/all_to_all | solution.py:83
  49.3 0.1 copy.80
  49.4 0.1 copy.75
  50.1 0.8 fusion.25
  51.0 27.8 %all-to-all-done.1 = bf16[2,16,16,1296]{3,2,0,1:T(8,128)(2,1)S(1)} async-done(((bf16[2,16,16,1296]{3,2,0,1:T(8,128)(2,1)}), bf16[2,16,16,1296]{3,2,0,1:T(8,128)(2,1)S(1)}, u32[]{:S(2)}, u32[]{:S(2)}) %all-to-all-start.1) | async-done | bytes 1327136 | tf_op jit(solution)/shard_map/all_to_all | solution.py:83
  78.9 2.1 %gather_fusion = bf16[512,1296]{1,0:T(8,128)(2,1)S(1)} fusion(bf16[512,1296]{1,0:T(8,128)(2,1)S(1)} %bitcast.47, s32[1024]{0:T(1024)S(1)} %pad_clamp_fusion.1), kind=kCustom, calls=%fused_computation | custom fusion | bytes 2656256 | tf_op jit(solution)/shard_map/jit(_take)/gather | solution.py:86
  81.1 2.2 %fusion.22 = bf16[4,1296,128]{1,0,2:T(4,128)(2,1)S(1)} fusion(bf16[4,128,1296]{2,1,0:T(8,128)(2,1)S(1)} %bitcast.54, pred[4,128]{0,1:T(8,128)(4,1)S(1)} %copy.75, bf16[4,128]{0,1:T(8,128)(2,1)S(1)} %copy.80), kind=kLoop, calls=%fused_computation.38 | loop fusion | flops 1327104 | bytes 2655744 | tf_op jit(solution)/shard_map/mul | solution.py:89
  83.2 0.6 fusion.48
  83.8 7.2 %collective-permute-start.3 = (bf16[4,1296,1]{1,0,2:T(4,128)(2,1)}, bf16[4,1296,1]{1,0,2:T(4,128)(2,1)}, u32[]{:S(2)}, u32[]{:S(2)}) collective-permute-start(bf16[4,1296,1]{1,0,2:T(4,128)(2,1)} %get-tuple-element.10), channel_id=1, source_target_pairs={{2,0},{4,2},{6,4},{8,6},{10,8},{12,10},{14,12},{16,14},{18,16},{20... | collective-permute-start | bytes 31112 | tf_op jit(solution)/shard_map/ppermute | solution.py:18
  91.0 1.9 %fusion.49 = (bf16[1,1296,128]{1,0,2:T(2,128)(2,1)S(1)}, bf16[1,1296,128]{1,0,2:T(2,128)(2,1)}) fusion(bf16[4,1296,128]{1,0,2:T(4,128)(2,1)S(1)} %fusion.22), kind=kLoop, calls=%fused_computation.103 | loop fusion | bytes 1327104 | tf_op jit(solution)/shard_map/slice | solution.py:15
  92.9 2.0 %copy.81 = bf16[4,1296,128]{2,0,1:T(4,128)(2,1)S(1)} copy(bf16[4,1296,128]{1,0,2:T(4,128)(2,1)S(1)} %fusion.22) | data formatting | bytes 2654208 | tf_op jit(solution)/shard_map/mul | solution.py:89
  94.9 2.8 %copy.86 = bf16[1,1296,128]{2,1,0:T(8,128)(2,1)} copy(bf16[1,1296,128]{1,0,2:T(2,128)(2,1)} %get-tuple-element.12) | data formatting | bytes 663552 | tf_op jit(solution)/shard_map/slice | solution.py:16
  97.7 1.3 collective-permute-start.7
  99.0 1.7 %copy.85 = bf16[1,1296,128]{2,1,0:T(8,128)(2,1)} copy(bf16[1,1296,128]{1,0,2:T(2,128)(2,1)S(1)} %get-tuple-element.11) | data formatting | bytes 663552 | tf_op jit(solution)/shard_map/slice | solution.py:15
  100.7 6.0 %collective-permute-start.6 = (bf16[1,1296,128]{2,1,0:T(8,128)(2,1)}, bf16[1,1296,128]{2,1,0:T(8,128)(2,1)}, u32[]{:S(2)}, u32[]{:S(2)}) collective-permute-start(bf16[1,1296,128]{2,1,0:T(8,128)(2,1)} %copy.85), channel_id=1, source_target_pairs={{0,1},{2,3},{4,5},{6,7},{8,9},{10,11},{12,13},{14,15},{16,17},{18,... | collective-permute-start | bytes 995336 | tf_op jit(solution)/shard_map/ppermute | solution.py:17
  106.7 0.8 concatenate.27
  107.5 2.6 %copy.84 = bf16[4,36,36,1]{3,0,2,1:T(4,128)(2,1)} copy(bf16[4,36,36,1]{2,1,0,3:T(8,128)(2,1)S(1)} %concatenate.27) | data formatting | bytes 20736 | tf_op jit(solution)/shard_map/concatenate | solution.py:19
  110.1 0.8 concatenate.26
  110.9 2.6 %copy.83 = bf16[4,36,36,1]{3,0,2,1:T(4,128)(2,1)} copy(bf16[4,36,36,1]{2,1,0,3:T(8,128)(2,1)S(1)} %concatenate.26) | data formatting | bytes 20736 | tf_op jit(solution)/shard_map/concatenate | solution.py:19
  113.5 4.8 %maximum_convert_fusion.1 = f32[4,36,36,130]{3,0,2,1:T(4,128)S(1)} fusion(bf16[4,36,36,1]{3,0,2,1:T(4,128)(2,1)} %copy.84, bf16[4,36,36,128]{3,0,2,1:T(4,128)(2,1)S(1)} %bitcast.52, bf16[4,36,36,1]{3,0,2,1:T(4,128)(2,1)} %copy.83), kind=kLoop, calls=%fused_computation.29 | loop fusion | flops 4043520 | bytes 4043520 | tf_op jit(solution)/shard_map/convert_element_type | solution.py:100
  118.3 5.6 %fusion.2 = f32[4,36,36,129]{3,0,2,1:T(4,128)} fusion(f32[4,36,36,130]{3,0,2,1:T(4,128)S(1)} %maximum_convert_fusion.1, f32[4,129]{1,0:T(4,128)S(1)} %fusion.29, f32[36,36]{1,0:T(8,128)S(1)} %get-tuple-element.29, f32[4,129]{1,0:T(4,128)S(1)} %slice_multiply_fusion.1), kind=kLoop, calls=%fused_computation.8 | loop fusion | flops 4681152 | bytes 8034144 | tf_op jit(solution)/shard_map/mul | solution.py:109
  123.9 2.3 %copy.88 = bf16[1,1296,128]{1,0,2:T(2,128)(2,1)S(1)} copy(bf16[1,1296,128]{2,1,0:T(8,128)(2,1)} %collective-permute-done.7) | data formatting | bytes 663552 | tf_op jit(solution)/shard_map/ppermute | solution.py:18
  126.2 2.9 %copy.87 = bf16[1,1296,128]{1,0,2:T(2,128)(2,1)} copy(bf16[1,1296,128]{2,1,0:T(8,128)(2,1)} %collective-permute-done.6) | data formatting | bytes 663552 | tf_op jit(solution)/shard_map/ppermute | solution.py:17
  129.1 3.4 %maximum_convert_fusion = f32[6,1296,128]{1,0,2:T(8,128)S(1)} fusion(bf16[1,1296,128]{1,0,2:T(2,128)(2,1)S(1)} %copy.88, bf16[4,1296,128]{1,0,2:T(4,128)(2,1)S(1)} %fusion.22, bf16[1,1296,128]{1,0,2:T(2,128)(2,1)} %copy.87), kind=kLoop, calls=%fused_computation.24 | loop fusion | flops 5971968 | bytes 5971968 | tf_op jit(solution)/shard_map/convert_element_type | solution.py:101
  132.5 5.0 %fusion.47 = (f32[5,1296,128]{1,0,2:T(8,128)}, f32[5,1296,128]{1,0,2:T(8,128)}) fusion(f32[6,1296,128]{1,0,2:T(8,128)S(1)} %maximum_convert_fusion), kind=kLoop, calls=%fused_computation.101 | loop fusion | bytes 13271040 | tf_op jit(solution)/shard_map/slice | solution.py:118
  137.5 6.3 %copy.89 = f32[5,1296,128]{2,0,1:T(8,128)} copy(f32[5,1296,128]{1,0,2:T(8,128)} %get-tuple-element.8) | data formatting | bytes 6635520 | tf_op jit(solution)/shard_map/slice | solution.py:118
  143.8 6.4 %copy.90 = f32[5,1296,128]{2,0,1:T(8,128)} copy(f32[5,1296,128]{1,0,2:T(8,128)} %get-tuple-element.7) | data formatting | bytes 6635520 | tf_op jit(solution)/shard_map/slice | solution.py:118
  150.2 5.5 %fusion.6 = f32[5,36,36,128]{3,0,2,1:T(8,128)S(1)} fusion(f32[5,36,36,128]{3,0,2,1:T(8,128)} %bitcast.50, f32[5,36,36,128]{3,0,2,1:T(8,128)} %bitcast.51, f32[5,128]{1,0:T(8,128)S(1)} %get-tuple-element.17, f32[36,36]{1,0:T(8,128)S(1)} %get-tuple-element.30, f32[5,128]{1,0:T(8,128)S(1)} %get-tuple-element.16), kind=kLoop, calls=%fused_computation.12 | loop fusion | flops 5806080 | bytes 9963584 | tf_op jit(solution)/shard_map/mul | solution.py:117
  155.7 2.1 %fusion.15 = f32[4,36,36,128]{3,0,2,1:T(4,128)S(1)} fusion(f32[5,36,36,128]{3,0,2,1:T(8,128)S(1)} %fusion.6, f32[4,36,36,129]{3,0,2,1:T(4,128)S(1)} %bitcast.49, bf16[4,36,36,128]{3,0,2,1:T(4,128)(2,1)S(1)} %bitcast.53), kind=kLoop, calls=%fused_computation.26 | loop fusion | flops 3317760 | bytes 14598144 | tf_op jit(solution)/shard_map/sub | solution.py:121
  157.8 0.2 slice.240
  158.0 0.7 copy-done
  158.7 1.0 fusion.17
  159.6 0.2 slice.243
  159.9 2.1 %fusion.23 = bf16[36,36,4,128]{3,2,1,0:T(4,128)(2,1)} fusion(f32[4,128]{1,0:T(4,128)S(1)} %get-tuple-element.27, f32[4,36,36,128]{3,0,2,1:T(4,128)S(1)} %fusion.15, f32[4,36,36,128]{3,0,2,1:T(4,128)S(1)} %fusion.17, f32[4,36,35,128]{3,0,2,1:T(4,128)S(1)} %slice.243, f32[4,36,1,128]{3,0,2,1:T(4,128)S(1)} %slice.242), kind=kLoop, calls=%fused_computation.39 | loop fusion | flops 3317760 | bytes 9291776 | tf_op jit(solution)/shard_map/transpose | solution.py:140
  (63 shorter events, 1.2 us)
Async XLA Ops:
  6.8 5.9 %copy-start.4 = (s32[4,128]{1,0:T(4,128)S(1)}, s32[4,128]{1,0:T(4,128)}, u32[]{:S(2)}) copy-start(s32[4,128]{1,0:T(4,128)} %param.15) | copy-start | bytes 6148
  6.8 5.9 %copy-start.3 = (bf16[2,1,8,128]{3,2,1,0:T(8,128)(2,1)S(1)}, bf16[2,1,8,128]{3,2,1,0:T(8,128)(2,1)}, u32[]{:S(2)}) copy-start(bf16[2,1,8,128]{3,2,1,0:T(8,128)(2,1)} %param.11) | copy-start | bytes 12292
  6.8 28.6 %copy-start.5 = (s32[4,1]{0,1:T(1,128)S(1)}, s32[4,1]{0,1:T(1,128)}, u32[]{:S(2)}) copy-start(s32[4,1]{0,1:T(1,128)} %param.13) | copy-start | bytes 52
  6.8 28.6 %copy-start.6 = (s32[4,1]{0,1:T(1,128)S(1)}, s32[4,1]{0,1:T(1,128)}, u32[]{:S(2)}) copy-start(s32[4,1]{0,1:T(1,128)} %param.12) | copy-start | bytes 52
  6.8 35.7 %copy-start.2 = (s32[4,128]{1,0:T(4,128)S(1)}, s32[4,128]{1,0:T(4,128)}, u32[]{:S(2)}) copy-start(s32[4,128]{1,0:T(4,128)} %param.14) | copy-start | bytes 6148
  8.4 34.2 %all-to-all-start = ((bf16[2,16,16,1296]{3,2,1,0:T(8,128)(2,1)}), bf16[2,16,16,1296]{3,2,1,0:T(8,128)(2,1)S(1)}, u32[]{:S(2)}, u32[]{:S(2)}) async-start(bf16[2,16,16,1296]{3,2,1,0:T(8,128)(2,1)} %bitcast.2), calls=%async_computation | async-start | bytes 2883584 | tf_op jit(solution)/shard_map/all_to_all | solution.py:82
  36.1 13.9 %collective-permute-start.5 = (bf16[1,3,128]{2,0,1:T(2,128)(2,1)S(1)}, bf16[1,3,128]{2,0,1:T(2,128)(2,1)S(1)}, u32[]{:S(2)}, u32[]{:S(2)}) collective-permute-start(bf16[1,3,128]{2,0,1:T(2,128)(2,1)S(1)} %get-tuple-element.23), channel_id=1, source_target_pairs={{1,0},{3,2},{5,4},{7,6},{9,8},{11,10},{13,12},{15,14},{17,16},{19,... | collective-permute-start | bytes 2312 | tf_op jit(solution)/shard_map/ppermute | solution.py:18
  37.4 12.6 %collective-permute-start.4 = (bf16[1,3,128]{2,0,1:T(2,128)(2,1)S(1)}, bf16[1,3,128]{2,0,1:T(2,128)(2,1)S(1)}, u32[]{:S(2)}, u32[]{:S(2)}) collective-permute-start(bf16[1,3,128]{2,0,1:T(2,128)(2,1)S(1)} %get-tuple-element.22), channel_id=1, source_target_pairs={{0,1},{2,3},{4,5},{6,7},{8,9},{10,11},{12,13},{14,15},{16,17},{18,... | collective-permute-start | bytes 2312 | tf_op jit(solution)/shard_map/ppermute | solution.py:17
  42.0 7.7 %collective-permute-start.1 = (bf16[4,3,1]{2,0,1:T(4,128)(2,1)S(1)}, bf16[4,3,1]{2,0,1:T(4,128)(2,1)S(1)}, u32[]{:S(2)}, u32[]{:S(2)}) collective-permute-start(bf16[4,3,1]{2,0,1:T(4,128)(2,1)S(1)} %get-tuple-element.21), channel_id=1, source_target_pairs={{2,0},{4,2},{6,4},{8,6},{10,8},{12,10},{14,12},{16,14},{18,16},{20... | collective-permute-start | bytes 80 | tf_op jit(solution)/shard_map/ppermute | solution.py:18
  42.1 7.6 %collective-permute-start = (bf16[4,3,1]{2,0,1:T(4,128)(2,1)S(1)}, bf16[4,3,1]{2,0,1:T(4,128)(2,1)S(1)}, u32[]{:S(2)}, u32[]{:S(2)}) collective-permute-start(bf16[4,3,1]{2,0,1:T(4,128)(2,1)S(1)} %get-tuple-element.20), channel_id=1, source_target_pairs={{0,2},{2,4},{4,6},{6,8},{8,10},{10,12},{12,14},{14,16},{16,18},{18... | collective-permute-start | bytes 80 | tf_op jit(solution)/shard_map/ppermute | solution.py:17
  43.9 34.9 %all-to-all-start.1 = ((bf16[2,16,16,1296]{3,2,0,1:T(8,128)(2,1)}), bf16[2,16,16,1296]{3,2,0,1:T(8,128)(2,1)S(1)}, u32[]{:S(2)}, u32[]{:S(2)}) async-start(bf16[2,16,16,1296]{3,2,0,1:T(8,128)(2,1)} %copy.77), calls=%async_computation.1 | async-start | bytes 2883584 | tf_op jit(solution)/shard_map/all_to_all | solution.py:83
  83.8 22.8 %collective-permute-start.3 = (bf16[4,1296,1]{1,0,2:T(4,128)(2,1)}, bf16[4,1296,1]{1,0,2:T(4,128)(2,1)}, u32[]{:S(2)}, u32[]{:S(2)}) collective-permute-start(bf16[4,1296,1]{1,0,2:T(4,128)(2,1)} %get-tuple-element.10), channel_id=1, source_target_pairs={{2,0},{4,2},{6,4},{8,6},{10,8},{12,10},{14,12},{16,14},{18,16},{20... | collective-permute-start | bytes 31112 | tf_op jit(solution)/shard_map/ppermute | solution.py:18
  91.0 19.1 %collective-permute-start.2 = (bf16[4,1296,1]{1,0,2:T(4,128)(2,1)}, bf16[4,1296,1]{1,0,2:T(4,128)(2,1)}, u32[]{:S(2)}, u32[]{:S(2)}) collective-permute-start(bf16[4,1296,1]{1,0,2:T(4,128)(2,1)} %get-tuple-element.9), channel_id=1, source_target_pairs={{0,2},{2,4},{4,6},{6,8},{8,10},{10,12},{12,14},{14,16},{16,18},{18... | collective-permute-start | bytes 31112 | tf_op jit(solution)/shard_map/ppermute | solution.py:17
  97.7 26.2 %collective-permute-start.7 = (bf16[1,1296,128]{2,1,0:T(8,128)(2,1)}, bf16[1,1296,128]{2,1,0:T(8,128)(2,1)}, u32[]{:S(2)}, u32[]{:S(2)}) collective-permute-start(bf16[1,1296,128]{2,1,0:T(8,128)(2,1)} %copy.86), channel_id=1, source_target_pairs={{1,0},{3,2},{5,4},{7,6},{9,8},{11,10},{13,12},{15,14},{17,16},{19,... | collective-permute-start | bytes 995336 | tf_op jit(solution)/shard_map/ppermute | solution.py:18
  100.7 25.5 %collective-permute-start.6 = (bf16[1,1296,128]{2,1,0:T(8,128)(2,1)}, bf16[1,1296,128]{2,1,0:T(8,128)(2,1)}, u32[]{:S(2)}, u32[]{:S(2)}) collective-permute-start(bf16[1,1296,128]{2,1,0:T(8,128)(2,1)} %copy.85), channel_id=1, source_target_pairs={{0,1},{2,3},{4,5},{6,7},{8,9},{10,11},{12,13},{14,15},{16,17},{18,... | collective-permute-start | bytes 995336 | tf_op jit(solution)/shard_map/ppermute | solution.py:17
  143.8 11.9 %slice-start = ((s8[5308416]{0:T(1024)(128)(4,1)}), s8[1114112]{0:T(1024)(128)(4,1)S(1)}, s32[]{:S(2)}) async-start(s8[5308416]{0:T(1024)(128)(4,1)} %bitcast.48), calls=%async_computation.2 | async-start | bytes 2228224
  150.2 5.5 %slice-start.1 = ((s8[5308416]{0:T(1024)(128)(4,1)}), s8[4194304]{0:T(1024)(128)(4,1)S(1)}, s32[]{:S(2)}) async-start(s8[5308416]{0:T(1024)(128)(4,1)} %bitcast.48), calls=%async_computation.3 | async-start | bytes 8388608
  157.7 0.9 copy-start
  157.8 0.9 copy-start.1
where the time goes:
time: 163 us; the launch traced here: 162 us
  local copies, waits for them, and re-layouts  46.7 us (29%)
  other arithmetic  34 us (21%)
  starting transfers between devices  30.4 us (19%)
  waiting for transfers between devices  27.8 us (17%)
  blocking collectives  22.7 us (14%)
    all_to_all x1, waiting for transfers between devices, body(): lax.all_to_all(section, 'lon', split_axis=1, concat_axis=1, tiled=True)  27.8 us
    all_gather x1, blocking collectives, body(): piece = lax.all_gather(ocean_current, 'lon', axis=2, tiled=True)  22.7 us
    slice x2, local copies, waits for them, and re-layouts, body(): tall[1:]  11.4 us
    ppermute x4, starting transfers between devices, with_halo(): before = lax.ppermute(last, axis, up)  11 us
    ppermute x4, starting transfers between devices, with_halo(): after = lax.ppermute(leading, axis, down)  9.73 us
    concatenate x4, local copies, waits for them, and re-layouts, with_halo(): shard = jnp.concatenate([before, shard, after], axis=dim)  6.81 us
    slice x1, local copies, waits for them, and re-layouts, body(): tall[:-1]  6.3 us
    mul x1, other arithmetic, body(): open_x[:, None, None, :]  5.55 us
  transfers between devices with their start and end apart: 10, of which 1 were waited for; matrix products, arithmetic and copies ran while one was open for 20% of the time, Pallas kernels for 0%

commit v1 on v0

v1 whole, which is shorter than its diff:
```python
import functools

import jax
import jax.numpy as jnp
import numpy as np
from jax import lax
from jax.experimental import pallas as pl
from jax.experimental.pallas import tpu as pltpu
from jax.sharding import PartitionSpec as P

fastest = 0.53
turn_scale = 2.5

VMEM = pl.BlockSpec(memory_space=pltpu.VMEM)
SMEM = pl.BlockSpec(memory_space=pltpu.SMEM)


def tables(freqs, dirs):
    ratio = 1.1 ** np.arange(freqs)
    spacing = 2.0 * np.pi / dirs
    theta = (np.arange(dirs) + 0.5) * spacing
    facing = (np.arange(dirs) + 1.0) * spacing
    f32 = np.float32
    return dict(
        group=(fastest / ratio).astype(f32),
        slow=(ratio / 44.6).astype(f32),
        rel=(ratio / ratio[freqs - 1]).astype(f32),
        cosd=np.cos(theta).astype(f32),
        sind=np.sin(theta).astype(f32),
        fcos=np.cos(facing).astype(f32),
        fsin=np.sin(facing).astype(f32),
    )


def source_kernel(slow_ref, rel_ref, spec_ref, u_ref, v_ref, trig_ref, out_ref):
    freqs, dirs, points = spec_ref.shape

    def add(f, acc):
        return acc + spec_ref[f].astype(jnp.float32)

    acc = lax.fori_loop(0, freqs, add, jnp.zeros((dirs, points), jnp.float32), unroll=4)
    mean = jnp.sum(acc, axis=0, keepdims=True) / (freqs * dirs)
    base = 0.3 * (mean / 0.5) ** 2
    proj = u_ref[...] * trig_ref[:, 0:1] + v_ref[...] * trig_ref[:, 1:2]

    def one(f, carry):
        drive = jnp.maximum(proj * slow_ref[f] - 1.0, 0.0)
        gain = 0.5 * jnp.tanh(0.2 * drive)
        grown = spec_ref[f].astype(jnp.float32) * jnp.exp(gain - rel_ref[f] * base)
        out_ref[f] = grown.astype(jnp.bfloat16)
        return carry

    lax.fori_loop(0, freqs, one, 0, unroll=2)


def source(tab, spec, wind_u, wind_v):
    trig = np.stack([tab["cosd"], tab["sind"]], axis=1)
    return pl.pallas_call(
        source_kernel,
        out_shape=jax.ShapeDtypeStruct(spec.shape, jnp.bfloat16),
        in_specs=[SMEM, SMEM, VMEM, VMEM, VMEM, VMEM],
        out_specs=VMEM,
        name="source",
    )(tab["slow"], tab["rel"], spec, wind_u[None], wind_v[None], trig)


def regroup_kernel(recv_ref, cell_ref, mask_ref, want_ref, ocean_ref, tile_ref, rows_ref, cols_ref, aux_ref):
    points, spectral = recv_ref.shape
    lat_rows, lon_cells = cell_ref.shape
    cell = cell_ref[...]
    mask = mask_ref[...]
    index = lax.broadcasted_iota(jnp.int32, (points, lon_cells), 0)
    hots = [
        jnp.where((index == cell[y : y + 1]) & (mask[y : y + 1] > 0), 1.0, 0.0).astype(jnp.bfloat16)
        for y in range(lat_rows)
    ]
    hot = jnp.concatenate(hots, axis=1)
    recv = recv_ref[...]
    dims = (((0,), (0,)), ((), ()))
    tile = lax.dot_general(recv, hot, dims, preferred_element_type=jnp.float32).astype(jnp.bfloat16)
    tile_ref[...] = tile
    blocks = ocean_ref.shape[1]
    pick = (lax.broadcasted_iota(jnp.int32, (lat_rows, blocks), 1) == want_ref[...]).astype(jnp.bfloat16)
    u = jnp.dot(pick, ocean_ref[0], preferred_element_type=jnp.float32)
    v = jnp.dot(pick, ocean_ref[1], preferred_element_type=jnp.float32)
    sea = mask.astype(jnp.float32)
    aux_ref[0] = u
    aux_ref[1] = v
    aux_ref[2] = sea
    for i, y in enumerate((0, lat_rows - 1)):
        rows_ref[i, :spectral] = tile[:, y * lon_cells : (y + 1) * lon_cells]
        extra = jnp.concatenate(
            [u[y : y + 1], v[y : y + 1], sea[y : y + 1], jnp.zeros((5, lon_cells), jnp.float32)], axis=0
        )
        rows_ref[i, spectral:] = extra.astype(jnp.bfloat16)
    lanes = lax.broadcasted_iota(jnp.int32, (lat_rows, points), 1)
    pad = cols_ref.shape[2] - spectral
    spot = lax.broadcasted_iota(jnp.int32, (lat_rows, pad), 1)
    for i, x in enumerate((0, lon_cells - 1)):
        edge = jnp.where((lanes == cell[:, x : x + 1]) & (mask[:, x : x + 1] > 0), 1.0, 0.0).astype(jnp.bfloat16)
        values = jnp.dot(edge, recv, preferred_element_type=jnp.float32)
        extra = jnp.where(
            spot == 0, u[:, x : x + 1], jnp.where(spot == 1, v[:, x : x + 1], jnp.where(spot == 2, sea[:, x : x + 1], 0.0))
        )
        cols_ref[i] = jnp.concatenate([values, extra], axis=1).astype(jnp.bfloat16)


def regroup(recv, cell, mask, want, ocean):
    points, spectral = recv.shape
    lat_rows, lon_cells = cell.shape
    wide = -(-(spectral + 3) // 128) * 128
    return pl.pallas_call(
        regroup_kernel,
        out_shape=(
            jax.ShapeDtypeStruct((spectral, points), jnp.bfloat16),
            jax.ShapeDtypeStruct((2, spectral + 8, lon_cells), jnp.bfloat16),
            jax.ShapeDtypeStruct((2, lat_rows, wide), jnp.bfloat16),
            jax.ShapeDtypeStruct((3, lat_rows, lon_cells), jnp.float32),
        ),
        in_specs=[VMEM] * 5,
        out_specs=(VMEM,) * 4,
        name="regroup",
    )(recv, cell, mask, want, ocean)


def upwind(speed, here, there):
    return jnp.where(speed > 0.0, here, there) * speed


def step_kernel(group_ref, tile_ref, south_ref, north_ref, west_ref, east_ref, cols_ref, aux_ref, trig_ref, freq_ref, out_ref, halo, turns, lay):
    spectral = tile_ref.shape[0]
    rows, lanes = turns.shape[1], aux_ref.shape[2]
    lat_rows = aux_ref.shape[1]
    dirs = rows // 2
    f32 = jnp.float32
    u, v, sea = aux_ref[0], aux_ref[1], aux_ref[2]
    lane = lax.broadcasted_iota(jnp.int32, (lat_rows, lanes), 1)
    west = west_ref[...].astype(f32)
    east = east_ref[...].astype(f32)

    def sides(a, i):
        at = spectral + i
        right = jnp.where(lane == lanes - 1, east[:, at : at + 1], pltpu.roll(a, lanes - 1, 1))
        left = jnp.where(lane == 0, west[:, at : at + 1], pltpu.roll(a, 1, 1))
        return left, right

    uw, ue = sides(u, 0)
    vw, ve = sides(v, 1)
    _, me = sides(sea, 2)
    open_x = sea * me
    face_u = 0.5 * (u + ue)
    below = south_ref[spectral : spectral + 8].astype(f32)
    above = north_ref[spectral : spectral + 8].astype(f32)
    ut = jnp.concatenate([below[0:1], u, above[0:1]], axis=0)
    vt = jnp.concatenate([below[1:2], v, above[1:2]], axis=0)
    mt = jnp.concatenate([below[2:3], sea, above[2:3]], axis=0)
    open_y = mt[:-1] * mt[1:]
    face_v = 0.5 * (vt[:-1] + vt[1:])
    ux = 0.5 * (ue - uw)
    vx = 0.5 * (ve - vw)
    uy = 0.5 * (ut[2:] - ut[:-2])
    vy = 0.5 * (vt[2:] - vt[:-2])
    fc, fs = trig_ref[:, 2:3], trig_ref[:, 3:4]
    for y in range(lat_rows):
        sl = slice(y, y + 1)
        turns[y] = turn_scale * (fs * fc * (ux[sl] - vy[sl]) + fs * fs * uy[sl] - fc * fc * vx[sl])
    own = cols_ref[0, :, :spectral].astype(f32)
    wide_u = west[:, spectral : spectral + 1]
    speed = freq_ref[0:1] + 0.5 * (wide_u + u[:, 0:1])
    flux_w = (west[:, spectral + 2 : spectral + 3] * sea[:, 0:1]) * upwind(speed, west[:, :spectral], own)
    hi = flux_w.astype(jnp.bfloat16)
    rest = flux_w - hi.astype(f32)
    mid = rest.astype(jnp.bfloat16)
    low = (rest - mid.astype(f32)).astype(jnp.bfloat16)
    left = jnp.concatenate([hi, mid, low, east_ref[:, :spectral]], axis=0)
    total = lat_rows * lanes
    j = lax.broadcasted_iota(jnp.int32, (4 * lat_rows, total), 0)
    c = lax.broadcasted_iota(jnp.int32, (4 * lat_rows, total), 1)
    part, jy = j // lat_rows, j % lat_rows
    place = jnp.where(c == jy * lanes + jnp.where(part == 3, lanes - 1, 0), 1.0, 0.0).astype(jnp.bfloat16)
    halo[...] = lax.dot_general(left, place, (((0,), (0,)), ((), ())), preferred_element_type=f32)

    row = lax.broadcasted_iota(jnp.int32, (rows, lanes), 0)
    full_lane = lax.broadcasted_iota(jnp.int32, (rows, lanes), 1)
    is_last, is_first = full_lane == lanes - 1, full_lane == 0
    top = row < dirs
    seam_up = (row == dirs - 1) | (row == rows - 1)
    seam_down = (row == 0) | (row == dirs)
    cosd, sind = trig_ref[:, 0:1], trig_ref[:, 1:2]

    def pair(i, carry):
        at = pl.multiple_of(i * rows, 8)
        sl = pl.ds(at, rows)
        speed_f = jnp.where(top, group_ref[2 * i], group_ref[2 * i + 1])
        gc = speed_f * cosd
        gs = speed_f * sind
        value = [tile_ref[sl, y * lanes : (y + 1) * lanes].astype(f32) for y in range(lat_rows)]
        below_v = south_ref[sl, :].astype(f32)
        above_v = north_ref[sl, :].astype(f32)
        flux_s = None
        for y in range(lat_rows + 1):
            lower = below_v if y == 0 else value[y - 1]
            upper = above_v if y == lat_rows else value[y]
            cy = gs + face_v[y : y + 1]
            flux_n = open_y[y : y + 1] * upwind(cy, lower, upper)
            if y > 0:
                k = y - 1
                e = value[k]
                edge = halo[sl, k * lanes : (k + 1) * lanes]
                ee = jnp.where(is_last, edge, pltpu.roll(e, lanes - 1, 1))
                cx = gc + face_u[k : k + 1]
                fx = open_x[k : k + 1] * upwind(cx, e, ee)
                fw = jnp.where(is_first, edge, pltpu.roll(fx, 1, 1))
                moved = e - (fx - fw) - (flux_n - flux_s)
                up = jnp.where(seam_up, pltpu.roll(moved, dirs - 1, 0), pltpu.roll(moved, rows - 1, 0))
                g = upwind(turns[k], moved, up)
                gp = jnp.where(seam_down, pltpu.roll(g, dirs + 1, 0), pltpu.roll(g, 1, 0))
                lay[pl.ds(k, rows, stride=lat_rows), :] = (moved - (g - gp)) * sea[k : k + 1]
            flux_s = flux_n
        out_ref[pl.ds(pl.multiple_of(at * lat_rows, 8), rows * lat_rows), :] = lay[...].astype(jnp.bfloat16)
        return carry

    lax.fori_loop(0, spectral // rows, pair, 0)


def step(tab, tile, south, north, west, east, cols, aux):
    spectral, points = tile.shape
    freqs, dirs = tab["group"].shape[0], tab["cosd"].shape[0]
    _, lat_rows, lon_cells = aux.shape
    trig = np.tile(np.stack([tab["cosd"], tab["sind"], tab["fcos"], tab["fsin"]], axis=1), (2, 1))
    freq = np.outer(tab["group"], tab["cosd"]).reshape(1, spectral)
    return pl.pallas_call(
        step_kernel,
        out_shape=jax.ShapeDtypeStruct((spectral * lat_rows, lon_cells), jnp.bfloat16),
        in_specs=[SMEM] + [VMEM] * 9,
        out_specs=VMEM,
        scratch_shapes=[
            pltpu.VMEM((spectral, points), jnp.float32),
            pltpu.VMEM((lat_rows, 2 * dirs, lon_cells), jnp.float32),
            pltpu.VMEM((2 * dirs * lat_rows, lon_cells), jnp.float32),
        ],
        name="step",
    )(tab["group"], tile, south, north, west, east, cols, aux, trig, freq)


def body(spec_pts, wind_u, wind_v, ocean_current, block_owner, block_slot, cell_source, land_mask):
    freqs, dirs, points = spec_pts.shape
    lat_rows, lon_cells = cell_source.shape
    n_lon, n_lat = lax.axis_size("lon"), lax.axis_size("lat")
    per_dest = points // (n_lon * n_lat)
    capacity = ocean_current.shape[2]
    spectral = freqs * dirs
    tab = tables(freqs, dirs)
    everyone = ("lon", "lat")

    want = block_owner * capacity + block_slot
    ocean = lax.all_gather(ocean_current[:, 0], "lon", axis=1, tiled=True)
    sourced = source(tab, spec_pts, wind_u, wind_v)
    packed = sourced.reshape(spectral, points).T.reshape(n_lat, n_lon, per_dest, spectral)
    packed = packed.transpose(1, 0, 2, 3).reshape(n_lon * n_lat, per_dest, spectral)
    got = lax.all_to_all(packed, everyone, split_axis=0, concat_axis=0, tiled=True)
    recv = got.reshape(points, spectral)
    s, r = cell_source // per_dest, cell_source % per_dest
    cell = ((s % n_lon) * n_lat + s // n_lon) * per_dest + r
    tile, rows, cols, aux = regroup(recv, cell, land_mask, want, ocean)
    right = [(i, (i + 1) % n_lon) for i in range(n_lon)]
    left = [(j, i) for i, j in right]
    west = lax.ppermute(cols[1], "lon", right)
    east = lax.ppermute(cols[0], "lon", left)
    up = [(i, i + 1) for i in range(n_lat - 1)]
    down = [(j, i) for i, j in up]
    south = lax.ppermute(rows[1], "lat", up)
    north = lax.ppermute(rows[0], "lat", down)
    out = step(tab, tile, south, north, west, east, cols, aux)
    return out.reshape(freqs, dirs, lat_rows, lon_cells)


def solution(mesh):
    return jax.shard_map(
        body,
        mesh=mesh,
        in_specs=(
            P(None, None, ("lon", "lat")),
            P(("lon", "lat")),
            P(("lon", "lat")),
            P(None, "lat", "lon", None),
            P("lat", "lon"),
            P("lat", "lon"),
            P("lat", "lon"),
            P("lat", "lon"),
        ),
        out_specs=P(None, None, "lat", "lon"),
        check_vma=False,
    )
```

time: 163 us -> 91 us (0.56)
  local copies, waits for them, and re-layouts: 46.7 us -> 8.25 us
  other arithmetic: 34 us -> 1.21 us
  waiting for transfers between devices: 27.8 us -> 5.81 us
  blocking collectives: 22.7 us -> 40.3 us
  Pallas kernels: 0 us -> 15.8 us
  starting transfers between devices: 30.4 us -> 19.1 us
    all_to_all x2 -> x1, waiting for transfers between devices: 27.8 us -> 0.01 us  [body(): lax.all_to_all(packed, everyone, split_axis=0, concat_axis=0, tiled=True)]
    slice x15 -> x0, local copies, waits for them, and re-layouts: 25.7 us -> none  [the longest x2 11.4 us: body(): tall[1:]]
    all_gather x1, blocking collectives: 22.7 us -> 40.3 us  [body(): ocean = lax.all_gather(ocean_current[:, 0], 'lon', axis=1, tiled=True)]
    pallas_call x0 -> x3, Pallas kernels: none -> 15.8 us  [the longest x1 8 us: step(): pl.pallas_call(step_kernel, out_shape=jax.ShapeDtypeStruct((spectral * la...]
    mul x13 -> x1, other arithmetic: 14.3 us -> 0.01 us  [body(): want = block_owner * capacity + block_slot]
    convert_element_type x6 -> x0, other arithmetic: 10.9 us -> none  [the longest x1 4.83 us: body(): wide_tile.astype(jnp.float32).reshape(lat_rows, freqs, dirs, lon_cells + 2)]
    ppermute x8 -> x4, starting transfers between devices: 20.8 us -> 11.8 us  [the longest x1 5.93 us: body(): east = lax.ppermute(cols[0], 'lon', left)]
    concatenate x4 -> x0, local copies, waits for them, and re-layouts: 6.81 us -> none  [with_halo(): shard = jnp.concatenate([before, shard, after], axis=dim)]
  transfers between devices with their start and end apart: 10 -> 5, of which waited for: 1 -> 2; matrix products, arithmetic and copies ran while one was open for 20% -> 2% of each run, Pallas kernels for 0% -> 0%
where the time goes in v1:
time: 91 us; the launch traced here: 90.6 us
  blocking collectives  40.3 us (44%)
  starting transfers between devices  19.1 us (21%)
  Pallas kernels  15.8 us (17%)
  local copies, waits for them, and re-layouts  8.25 us (9%)
  waiting for transfers between devices  5.81 us (6%)
  other arithmetic  1.21 us (1%)
    all_gather x1, blocking collectives, body(): ocean = lax.all_gather(ocean_current[:, 0], 'lon', axis=1, tiled=True)  40.3 us
    pallas_call x1, Pallas kernels, step(): pl.pallas_call(step_kernel, out_shape=jax.ShapeDtypeStruct((spectral * la...  8 us
    all_to_all x1, starting transfers between devices, body(): lax.all_to_all(packed, everyone, split_axis=0, concat_axis=0, tiled=True)  7.33 us
    ppermute x1, starting transfers between devices, body(): east = lax.ppermute(cols[0], 'lon', left)  5.93 us
    ppermute x1, starting transfers between devices, body(): south = lax.ppermute(rows[1], 'lat', up)  4.58 us
    ppermute x1, waiting for transfers between devices, body(): west = lax.ppermute(cols[1], 'lon', right)  4.41 us
    pallas_call x1, Pallas kernels, source(): pl.pallas_call(source_kernel, out_shape=jax.ShapeDtypeStruct(spec.shape,...  4.23 us
    pallas_call x1, Pallas kernels, regroup(): pl.pallas_call(regroup_kernel, out_shape=(jax.ShapeDtypeStruct((spectral,...  3.56 us
  transfers between devices with their start and end apart: 5, of which 2 were waited for; matrix products, arithmetic and copies ran while one was open for 2% of the time, Pallas kernels for 0%

profile of v1, /device:TPU:0, one launch (start us, length us, event | category | flops | bytes accessed | tf_op | source)
XLA Modules:
  0.0 90.6 jit_solution(2639850432916924051)
XLA Ops:
  0.0 4.2 %source.1 = bf16[36,36,512]{2,1,0:T(8,128)(2,1)} custom-call(f32[36]{0:T(128)} %constant.57.clone.slow_ref, f32[36]{0:T(128)} %constant.58.clone.rel_ref, bf16[36,36,512]{2,1,0:T(8,128)(2,1)} %spec_ref.1, f32[1,512]{1,0:T(1,128)} %bitcast.24, f32[1,512]{1,0:T(1,128)} %bitcast.25, f32[36,2]{1,0:T(8,128)} %constant.59.clone.trig_ref), custom_call_target="tpu_custom_call" | custom-call | tf_op jit(solution)/shard_map/source/pallas_call | solution.py:58
  4.2 2.2 %reshape.15 = bf16[1296,512]{1,0:T(8,128)(2,1)S(1)} reshape(bf16[36,36,512]{2,1,0:T(8,128)(2,1)} %source.1) | data formatting | bytes 2654208 | tf_op jit(solution)/shard_map/reshape | solution.py:259
  6.5 0.8 copy.25
  7.3 1.2 %copy.26 = bf16[16,2,16,1296]{3,2,1,0:T(8,128)(2,1)} copy(bf16[16,2,16,1296]{3,2,0,1:T(8,128)(2,1)S(1)} %bitcast.21) | data formatting | bytes 2654208 | tf_op jit(solution)/shard_map/transpose | solution.py:260
  8.5 0.0 copy-start.8
  8.5 0.0 copy-start.7
  8.5 0.0 copy-start.5
  8.5 0.0 copy-start.6
  8.5 7.3 %all-to-all-start = ((bf16[32,16,1296]{2,1,0:T(8,128)(2,1)}), bf16[32,16,1296]{2,1,0:T(8,128)(2,1)S(1)}, u32[]{:S(2)}, u32[]{:S(2)}) async-start(bf16[32,16,1296]{2,1,0:T(8,128)(2,1)} %bitcast.5), calls=%async_computation | async-start | bytes 2883584 | tf_op jit(solution)/shard_map/all_to_all | solution.py:261
  15.9 0.0 copy-done.8
  15.9 0.1 copy.28
  16.0 0.0 copy-done.7
  16.0 0.1 copy.29
  16.1 0.6 add.25.want_ref
  16.7 0.0 copy-done.5
  16.7 40.3 %all-gather = bf16[2,1,128,128]{3,2,0,1:T(8,128)(2,1)} all-gather(bf16[2,1,8,128]{3,2,0,1:T(8,128)(2,1)S(1)} %bitcast.23), channel_id=2, replica_groups=mesh['lon'=16,'lat'=2] {'lon'}, dimensions={2}, use_global_device_ids=true | all-gather | bytes 69632 | tf_op jit(solution)/shard_map/all_gather | solution.py:257
  56.9 0.0 copy-done.6
  56.9 0.6 fusion.3.cell_ref
  57.5 0.0 all-to-all-done
  57.5 0.0 copy-start
  57.5 1.1 %copy-done = bf16[32,16,1296]{2,1,0:T(8,128)(2,1)} copy-done((bf16[32,16,1296]{2,1,0:T(8,128)(2,1)}, bf16[32,16,1296]{2,1,0:T(8,128)(2,1)S(1)}, u32[]{:S(2)}) %copy-start) | copy-done | bytes 1327128
  58.6 3.6 %regroup.1 = (bf16[1296,512]{1,0:T(8,128)(2,1)}, bf16[2,1304,128]{2,1,0:T(8,128)(2,1)}, bf16[2,4,1408]{2,1,0:T(4,128)(2,1)}, f32[3,4,128]{2,1,0:T(4,128)}) custom-call(bf16[512,1296]{1,0:T(8,128)(2,1)} %bitcast.20, s32[4,128]{1,0:T(4,128)} %fusion.3.cell_ref, s32[4,128]{1,0:T(4,128)} %mask_ref.1, s32[4,1]{1,0:T(4,128)} %add.25.want_ref, ...), custom_call_target="tpu_custom_call" | custom-call | tf_op jit(solution)/shard_map/regroup/pallas_call | solution.py:112
  62.2 1.1 %slice_bitcast_fusion = (bf16[1304,128]{1,0:T(8,128)(2,1)S(1)}, bf16[1304,128]{1,0:T(8,128)(2,1)S(1)}) fusion(bf16[2,1304,128]{2,1,0:T(8,128)(2,1)} %get-tuple-element.10), kind=kLoop, calls=%fused_computation | loop fusion | bytes 1335296 | tf_op jit(solution)/shard_map/squeeze | solution.py:273
  63.3 1.3 %collective-permute-start.1 = (bf16[1304,128]{1,0:T(8,128)(2,1)S(1)}, bf16[1304,128]{1,0:T(8,128)(2,1)S(1)}, u32[]{:S(2)}, u32[]{:S(2)}) collective-permute-start(bf16[1304,128]{1,0:T(8,128)(2,1)S(1)} %get-tuple-element.13), channel_id=1, source_target_pairs={{1,0},{3,2},{5,4},{7,6},{9,8},{11,10},{13,12},{15,14},{17,16},{19,... | collective-permute-start | bytes 1001480 | tf_op jit(solution)/shard_map/ppermute | solution.py:273
  64.6 4.6 %collective-permute-start = (bf16[1304,128]{1,0:T(8,128)(2,1)S(1)}, bf16[1304,128]{1,0:T(8,128)(2,1)S(1)}, u32[]{:S(2)}, u32[]{:S(2)}) collective-permute-start(bf16[1304,128]{1,0:T(8,128)(2,1)S(1)} %get-tuple-element.14), channel_id=1, source_target_pairs={{0,1},{2,3},{4,5},{6,7},{8,9},{10,11},{12,13},{14,15},{16,17},{18,... | collective-permute-start | bytes 1001480 | tf_op jit(solution)/shard_map/ppermute | solution.py:272
  69.2 0.7 slice_bitcast_fusion.2
  70.0 5.9 %collective-permute-start.3 = (bf16[4,1408]{1,0:T(4,128)(2,1)S(1)}, bf16[4,1408]{1,0:T(4,128)(2,1)S(1)}, u32[]{:S(2)}, u32[]{:S(2)}) collective-permute-start(bf16[4,1408]{1,0:T(4,128)(2,1)S(1)} %get-tuple-element.15), channel_id=1, source_target_pairs={{2,0},{4,2},{6,4},{8,6},{10,8},{12,10},{14,12},{16,14},{18,16},{20... | collective-permute-start | bytes 33800 | tf_op jit(solution)/shard_map/ppermute | solution.py:269
  75.9 0.0 collective-permute-start.2
  75.9 1.4 %collective-permute-done.3.east_ref = bf16[4,1408]{1,0:T(4,128)(2,1)S(1)} collective-permute-done((bf16[4,1408]{1,0:T(4,128)(2,1)S(1)}, bf16[4,1408]{1,0:T(4,128)(2,1)S(1)}, u32[]{:S(2)}, u32[]{:S(2)}) %collective-permute-start.3) | collective-permute-done | bytes 11296 | tf_op jit(solution)/shard_map/ppermute | solution.py:269
  77.3 0.0 copy-start.3
  77.3 4.4 %collective-permute-done.2.west_ref = bf16[4,1408]{1,0:T(4,128)(2,1)S(1)} collective-permute-done((bf16[4,1408]{1,0:T(4,128)(2,1)S(1)}, bf16[4,1408]{1,0:T(4,128)(2,1)S(1)}, u32[]{:S(2)}, u32[]{:S(2)}) %collective-permute-start.2) | collective-permute-done | bytes 11296 | tf_op jit(solution)/shard_map/ppermute | solution.py:268
  81.7 0.0 copy-start.4
  81.7 0.0 collective-permute-done.1.north_ref
  81.7 0.0 copy-start.1
  81.7 0.0 collective-permute-done.south_ref
  81.7 0.0 copy-start.2
  81.7 0.0 copy-done.3
  81.7 0.6 copy-done.4
  82.3 0.1 copy-done.1
  82.4 0.1 copy-done.2
  82.5 8.0 %step.1 = bf16[5184,128]{1,0:T(8,128)(2,1)} custom-call(f32[36]{0:T(128)} %constant.60.clone.group_ref, bf16[1296,512]{1,0:T(8,128)(2,1)} %get-tuple-element.9.tile_ref, bf16[1304,128]{1,0:T(8,128)(2,1)} %copy-done.2, bf16[1304,128]{1,0:T(8,128)(2,1)} %copy-done.1, bf16[4,1408]{1,0:T(4,128)(2,1)} %copy-done.4, bf16[4,1408]{1,0:T(4,128)(2,1)} %copy-done.3, ...), custom_call_target="tpu_custom_call" | custom-call | tf_op jit(solution)/shard_map/step/pallas_call | solution.py:232
  (1 shorter events, 0.0 us)
Async XLA Ops:
  8.5 7.4 %copy-start.8 = (s32[4,1]{0,1:T(1,128)S(1)}, s32[4,1]{0,1:T(1,128)}, u32[]{:S(2)}) copy-start(s32[4,1]{0,1:T(1,128)} %param.18) | copy-start | bytes 52
  8.5 7.5 %copy-start.7 = (s32[4,1]{0,1:T(1,128)S(1)}, s32[4,1]{0,1:T(1,128)}, u32[]{:S(2)}) copy-start(s32[4,1]{0,1:T(1,128)} %param.19) | copy-start | bytes 52
  8.5 8.2 %copy-start.5 = (bf16[2,1,8,128]{3,2,1,0:T(8,128)(2,1)S(1)}, bf16[2,1,8,128]{3,2,1,0:T(8,128)(2,1)}, u32[]{:S(2)}) copy-start(bf16[2,1,8,128]{3,2,1,0:T(8,128)(2,1)} %param.17) | copy-start | bytes 12292
  8.5 48.4 %copy-start.6 = (s32[4,128]{1,0:T(4,128)S(1)}, s32[4,128]{1,0:T(4,128)}, u32[]{:S(2)}) copy-start(s32[4,128]{1,0:T(4,128)} %param.20) | copy-start | bytes 6148
  8.5 49.0 %all-to-all-start = ((bf16[32,16,1296]{2,1,0:T(8,128)(2,1)}), bf16[32,16,1296]{2,1,0:T(8,128)(2,1)S(1)}, u32[]{:S(2)}, u32[]{:S(2)}) async-start(bf16[32,16,1296]{2,1,0:T(8,128)(2,1)} %bitcast.5), calls=%async_computation | async-start | bytes 2883584 | tf_op jit(solution)/shard_map/all_to_all | solution.py:261
  57.5 1.1 %copy-start = (bf16[32,16,1296]{2,1,0:T(8,128)(2,1)}, bf16[32,16,1296]{2,1,0:T(8,128)(2,1)S(1)}, u32[]{:S(2)}) copy-start(bf16[32,16,1296]{2,1,0:T(8,128)(2,1)S(1)} %all-to-all-done) | copy-start | bytes 3981316
  63.3 18.4 %collective-permute-start.1 = (bf16[1304,128]{1,0:T(8,128)(2,1)S(1)}, bf16[1304,128]{1,0:T(8,128)(2,1)S(1)}, u32[]{:S(2)}, u32[]{:S(2)}) collective-permute-start(bf16[1304,128]{1,0:T(8,128)(2,1)S(1)} %get-tuple-element.13), channel_id=1, source_target_pairs={{1,0},{3,2},{5,4},{7,6},{9,8},{11,10},{13,12},{15,14},{17,16},{19,... | collective-permute-start | bytes 1001480 | tf_op jit(solution)/shard_map/ppermute | solution.py:273
  64.6 17.1 %collective-permute-start = (bf16[1304,128]{1,0:T(8,128)(2,1)S(1)}, bf16[1304,128]{1,0:T(8,128)(2,1)S(1)}, u32[]{:S(2)}, u32[]{:S(2)}) collective-permute-start(bf16[1304,128]{1,0:T(8,128)(2,1)S(1)} %get-tuple-element.14), channel_id=1, source_target_pairs={{0,1},{2,3},{4,5},{6,7},{8,9},{10,11},{12,13},{14,15},{16,17},{18,... | collective-permute-start | bytes 1001480 | tf_op jit(solution)/shard_map/ppermute | solution.py:272
  70.0 7.3 %collective-permute-start.3 = (bf16[4,1408]{1,0:T(4,128)(2,1)S(1)}, bf16[4,1408]{1,0:T(4,128)(2,1)S(1)}, u32[]{:S(2)}, u32[]{:S(2)}) collective-permute-start(bf16[4,1408]{1,0:T(4,128)(2,1)S(1)} %get-tuple-element.15), channel_id=1, source_target_pairs={{2,0},{4,2},{6,4},{8,6},{10,8},{12,10},{14,12},{16,14},{18,16},{20... | collective-permute-start | bytes 33800 | tf_op jit(solution)/shard_map/ppermute | solution.py:269
  75.9 5.8 %collective-permute-start.2 = (bf16[4,1408]{1,0:T(4,128)(2,1)S(1)}, bf16[4,1408]{1,0:T(4,128)(2,1)S(1)}, u32[]{:S(2)}, u32[]{:S(2)}) collective-permute-start(bf16[4,1408]{1,0:T(4,128)(2,1)S(1)} %get-tuple-element.16), channel_id=1, source_target_pairs={{0,2},{2,4},{4,6},{6,8},{8,10},{10,12},{12,14},{14,16},{16,18},{18... | collective-permute-start | bytes 33800 | tf_op jit(solution)/shard_map/ppermute | solution.py:268
  77.3 4.4 %copy-start.3 = (bf16[4,1408]{1,0:T(4,128)(2,1)}, bf16[4,1408]{1,0:T(4,128)(2,1)S(1)}, u32[]{:S(2)}) copy-start(bf16[4,1408]{1,0:T(4,128)(2,1)S(1)} %collective-permute-done.3.east_ref) | copy-start | bytes 33796
  81.7 0.6 copy-start.4
  81.7 0.7 copy-start.1
  81.7 0.8 copy-start.2

commit v2 on v1

--- a/solution.py
+++ b/solution.py
@@ -8,9 +8,11 @@
 from jax.experimental.pallas import tpu as pltpu
 from jax.sharding import PartitionSpec as P
 
+
 fastest = 0.53
 turn_scale = 2.5
 
+GRANT = pltpu.CompilerParams(vmem_limit_bytes=20 * 1024 * 1024)
 VMEM = pl.BlockSpec(memory_space=pltpu.VMEM)
 SMEM = pl.BlockSpec(memory_space=pltpu.SMEM)
 
@@ -61,6 +63,7 @@
         in_specs=[SMEM, SMEM, VMEM, VMEM, VMEM, VMEM],
         out_specs=VMEM,
         name="source",
+        compiler_params=GRANT,
     )(tab["slow"], tab["rel"], spec, wind_u[None], wind_v[None], trig)
 
 
@@ -120,23 +123,437 @@
         in_specs=[VMEM] * 5,
         out_specs=(VMEM,) * 4,
         name="regroup",
+        compiler_params=GRANT,
     )(recv, cell, mask, want, ocean)
+
+
+def grow_four(four, spec_ref, slow_ref, rel_ref, proj, base, first):
+    parts = []
+    for q in range(4):
+        f = first + 4 * four + q
+        drive = jnp.maximum(proj * slow_ref[f] - 1.0, 0.0)
+        gain = 0.5 * jnp.tanh(0.2 * drive)
+        parts.append(spec_ref[f].astype(jnp.float32) * jnp.exp(gain - rel_ref[f] * base))
+    return jnp.concatenate(parts, axis=0).astype(jnp.bfloat16)
+
+
+def one_hot(index, depth):
+    rows = lax.broadcasted_iota(jnp.int32, (depth, index.shape[1]), 0)
+    return jnp.where(rows == index, 1.0, 0.0).astype(jnp.bfloat16)
+
+
+class Route:
+    def __init__(self, grid, n_lat, per):
+        self.nz, self.nx, self.nc = grid
+        self.ny, self.per = n_lat, per
+        self.plane = self.nx * self.ny
+        self.points = self.nz * self.nx * self.nc * n_lat * per
+
+    def here(self):
+        t = lax.axis_index("lon")
+        return t // (self.nx * self.nc), t // self.nc % self.nx, t % self.nc, lax.axis_index("lat")
+
+    def source_lane(self, z, x, c, y):
+        n_lon = self.nz * self.nx * self.nc
+        return (y * n_lon + (z * self.nx + x) * self.nc + c) * self.per
+
+    def parts(self, sizes):
+        q = lax.broadcasted_iota(jnp.int32, (1, self.points), 1)
+        digits = []
+        for n in (self.per, *reversed(sizes)):
+            digits.append(q % n)
+            q = q // n
+        return digits[::-1]
+
+    def b1(self):
+        z, _, _, _ = self.here()
+        gz, yd, xd, cd, r = self.parts((self.nz, self.ny, self.nx, self.nc))
+        return self.source_lane((z + gz) % self.nz, xd, cd, yd) + r
+
+    def b2(self):
+        _, x, _, y = self.here()
+        gx, gy, gz, cd, r = self.parts((self.nx, self.ny, self.nz, self.nc))
+        xd, yd = (x + gx) % self.nx, (y + gy) % self.ny
+        return (((gz * self.ny + yd) * self.nx + xd) * self.nc + cd) * self.per + r
+
+    def b3(self):
+        _, _, c, _ = self.here()
+        gc, g, gz, r = self.parts((self.nc, self.plane, self.nz))
+        return ((g * self.nz + gz) * self.nc + (c + gc) % self.nc) * self.per + r
+
+    def a1(self):
+        _, _, c, _ = self.here()
+        gc, yd, zd, xd, r = self.parts((self.nc, self.ny, self.nz, self.nx))
+        return self.source_lane(zd, xd, (c + gc) % self.nc, yd) + r
+
+    def a2(self):
+        _, x, _, y = self.here()
+        gx, gy, gc, zd, r = self.parts((self.nx, self.ny, self.nc, self.nz))
+        xd, yd = (x + gx) % self.nx, (y + gy) % self.ny
+        return (((gc * self.ny + yd) * self.nz + zd) * self.nx + xd) * self.per + r
+
+    def a3(self):
+        z, _, _, _ = self.here()
+        gz, g, gc, r = self.parts((self.nz, self.plane, self.nc))
+        return ((g * self.nc + gc) * self.nz + (z + gz) % self.nz) * self.per + r
+
+    def split(self, cell):
+        z, x, c, y = self.here()
+        n_lon = self.nz * self.nx * self.nc
+        r, s = cell % self.per, cell // self.per
+        a, b = s % n_lon, s // n_lon
+        za, xa, ca = a // (self.nx * self.nc), a // self.nc % self.nx, a % self.nc
+        gz, gx = (z - za + self.nz) % self.nz, (x - xa + self.nx) % self.nx
+        gc, gy = (c - ca + self.nc) % self.nc, (y - b + self.ny) % self.ny
+        return gz, gx, gc, gy, r
+
+    def b_end(self, cell):
+        gz, gx, gc, gy, r = self.split(cell)
+        return ((gc * self.plane + gx * self.ny + gy) * self.nz + gz) * self.per + r
+
+    def a_end(self, cell):
+        gz, gx, gc, gy, r = self.split(cell)
+        return ((gz * self.plane + gx * self.ny + gy) * self.nc + gc) * self.per + r
+
+    def shift(self, axis_steps):
+        dz, dx, dc, dy = axis_steps
+        pairs = []
+        for z in range(self.nz):
+            for x in range(self.nx):
+                for c in range(self.nc):
+                    for y in range(self.ny):
+                        a = ((z + dz) % self.nz * self.nx + (x + dx) % self.nx) * self.nc + (c + dc) % self.nc
+                        here = ((z * self.nx + x) * self.nc + c) * self.ny + y
+                        pairs.append((here, a * self.ny + (y + dy) % self.ny))
+        return pairs
+
+
+def source_b_kernel(route, first, slow_ref, rel_ref, spec_ref, u_ref, v_ref, trig_ref, ocean_ref, *rest):
+    *out_refs, base_ref, hot = rest
+    freqs, dirs, points = spec_ref.shape
+    hot[...] = one_hot(route.b1(), points)
+
+    def add(f, acc):
+        return acc + spec_ref[f].astype(jnp.float32)
+
+    acc = lax.fori_loop(0, freqs, add, jnp.zeros((dirs, points), jnp.float32), unroll=4)
+    mean = jnp.sum(acc, axis=0, keepdims=True) / (freqs * dirs)
+    base = 0.3 * (mean / 0.5) ** 2
+    base_ref[...] = base
+    proj = u_ref[...] * trig_ref[:, 0:1] + v_ref[...] * trig_ref[:, 1:2]
+    size = 4 * dirs
+    rows, lanes = out_refs[0].shape
+
+    def four(i, carry):
+        grown = grow_four(i, spec_ref, slow_ref, rel_ref, proj, base, first)
+        moved = jnp.dot(grown, hot[...], preferred_element_type=jnp.float32).astype(jnp.bfloat16)
+        at = pl.ds(pl.multiple_of(i * size, 16), size)
+        for g, out in enumerate(out_refs):
+            out[at] = moved[:, g * lanes : (g + 1) * lanes]
+        return carry
+
+    lax.fori_loop(0, rows // size, four, 0)
+    for out in out_refs[1:]:
+        out[rows:] = ocean_ref[...]
+
+
+def source_a_kernel(route, first, slow_ref, rel_ref, spec_ref, u_ref, v_ref, trig_ref, base_ref, *rest):
+    *out_refs, hot = rest
+    _, dirs, points = spec_ref.shape
+    hot[...] = one_hot(route.a1(), points)
+    proj = u_ref[...] * trig_ref[:, 0:1] + v_ref[...] * trig_ref[:, 1:2]
+    base = base_ref[...]
+    size = 4 * dirs
+    rows, lanes = out_refs[0].shape
+
+    def four(i, carry):
+        grown = grow_four(i, spec_ref, slow_ref, rel_ref, proj, base, first)
+        moved = jnp.dot(grown, hot[...], preferred_element_type=jnp.float32).astype(jnp.bfloat16)
+        at = pl.ds(pl.multiple_of(i * size, 16), size)
+        for g, out in enumerate(out_refs):
+            out[at] = moved[:, g * lanes : (g + 1) * lanes]
+        return carry
+
+    lax.fori_loop(0, rows // size, four, 0)
+
+
+def bf16(*shape):
+    return jax.ShapeDtypeStruct(shape, jnp.bfloat16)
+
+
+def hot_scratch(points):
+    return [pltpu.VMEM((points, points), jnp.bfloat16)]
+
+
+def source_b(tab, route, first, count, spec, wind_u, wind_v, ocean):
+    _, dirs, points = spec.shape
+    trig = np.stack([tab["cosd"], tab["sind"]], axis=1)
+    k, lanes = count * dirs, points // route.nz
+    more = ocean.shape[0]
+    outs = [bf16(k, lanes)] + [bf16(k + more, lanes)] * (route.nz - 1)
+
+    def kernel(slow, rel, spec_ref, u, v, trig_ref, ocean_ref, *rest):
+        outs_ = rest[: route.nz]
+        own, sent = outs_[0], outs_[1:]
+        source_b_kernel(route, first, slow, rel, spec_ref, u, v, trig_ref, ocean_ref, own, *sent, *rest[route.nz :])
+
+    return pl.pallas_call(
+        kernel,
+        out_shape=(*outs, jax.ShapeDtypeStruct((1, points), jnp.float32)),
+        in_specs=[SMEM, SMEM] + [VMEM] * 5,
+        out_specs=(VMEM,) * (route.nz + 1),
+        scratch_shapes=hot_scratch(points),
+        name="source_b",
+        compiler_params=GRANT,
+    )(tab["slow"], tab["rel"], spec, wind_u[None], wind_v[None], trig, ocean)
+
+
+def source_a(tab, route, first, count, spec, wind_u, wind_v, base):
+    _, dirs, points = spec.shape
+    trig = np.stack([tab["cosd"], tab["sind"]], axis=1)
+    return pl.pallas_call(
+        functools.partial(source_a_kernel, route, first),
+        out_shape=(bf16(count * dirs, points // route.nc),) * route.nc,
+        in_specs=[SMEM, SMEM] + [VMEM] * 5,
+        out_specs=(VMEM,) * route.nc,
+        scratch_shapes=hot_scratch(points),
+        name="source_a",
+        compiler_params=GRANT,
+    )(tab["slow"], tab["rel"], spec, wind_u[None], wind_v[None], trig, base)
+
+
+def shuffle(index, size, ins, outs, points, n_in, n_out, extra=None):
+    return pl.pallas_call(
+        functools.partial(shuffle_body, index, size, n_in, len(ins), n_out, extra),
+        out_shape=tuple(outs),
+        in_specs=[VMEM] * len(ins),
+        out_specs=(VMEM,) * len(outs),
+        scratch_shapes=hot_scratch(points),
+        compiler_params=GRANT,
+    )(*ins)
+
+
+def shuffle_body(index, size, n_in, n_all, n_out, extra, *refs):
+    ins, hot = refs[:n_in], refs[-1]
+    others, outs = refs[n_in:n_all], refs[n_all:-1]
+    hot[...] = one_hot(index(), hot.shape[0])
+    rows = ins[0].shape[0]
+    lanes = outs[0].shape[1]
+
+    def block(i, carry):
+        at = pl.ds(pl.multiple_of(i * size, 16), size)
+        have = jnp.concatenate([r[at] for r in ins], axis=1)
+        moved = jnp.dot(have, hot[...], preferred_element_type=jnp.float32).astype(jnp.bfloat16)
+        for g in range(n_out):
+            outs[g][at] = moved[:, g * lanes : (g + 1) * lanes]
+        return carry
+
+    lax.fori_loop(0, rows // size, block, 0)
+    if extra:
+        extra(rows, ins, others, outs)
+
+
+def swap(parts, perms):
+    moved = []
+    for part, perm in zip(parts, perms):
+        moved.append(lax.ppermute(part, ("lon", "lat"), perm))
+    return moved
+
+
+def exchange_b(route, size, parts, ocean):
+    points, k = route.points, parts[0].shape[0]
+    nz, nx, ny, nc = route.nz, route.nx, route.ny, route.nc
+    more = ocean.shape[0]
+    lanes = points // nz
+    got = swap(parts[1:], [route.shift((d, 0, 0, 0)) for d in range(1, nz)])
+    steps = [(gx, gy) for gx in range(nx) for gy in range(ny)]
+    column = [i for i, (gx, gy) in enumerate(steps) if gy == 0]
+
+    def gather_z(rows, ins, others, outs):
+        blocks = [others[0][...]] + [r[rows:] for r in ins[1:]]
+        whole = jnp.concatenate(blocks, axis=0)
+        outs[-1][...] = whole
+        for i in column[1:]:
+            outs[i][rows:] = whole
+
+    wide = points // len(steps)
+    outs = [bf16(k + (nz * more if i in column[1:] else 0), wide) for i in range(len(steps))]
+    *parts, ocean_z = shuffle(
+        route.b2, size, [parts[0], *got, ocean], [*outs, bf16(nz * more, lanes)], points, nz, len(steps), gather_z
+    )
+    got = swap(parts[1:], [route.shift((0, gx, 0, gy)) for gx, gy in steps[1:]])
+
+    def gather_x(rows, ins, others, outs):
+        blocks = [others[0][...]] + [ins[i][rows:] for i in column[1:]]
+        whole = jnp.concatenate(blocks, axis=1)
+        outs[-1][...] = whole
+        for out in outs[1:nc]:
+            out[rows:] = whole
+
+    deep, side = nz * more, nx * lanes
+    outs = [bf16(k, points // nc)] + [bf16(k + deep, points // nc)] * (nc - 1) + [bf16(deep, side)]
+    keep, *sent, ocean_x = shuffle(route.b3, size, [parts[0], *got, ocean_z], outs, points, len(steps), nc, gather_x)
+    got = swap(sent, [route.shift((0, 0, d, 0)) for d in range(1, nc)])
+    return [keep, *got], ocean_x
+
+
+def exchange_a(route, size, parts):
+    points, k = route.points, parts[0].shape[0]
+    nz, nx, ny, nc = route.nz, route.nx, route.ny, route.nc
+    got = swap(parts[1:], [route.shift((0, 0, d, 0)) for d in range(1, nc)])
+    steps = [(gx, gy) for gx in range(nx) for gy in range(ny)]
+    outs = [bf16(k, points // len(steps))] * len(steps)
+    parts = shuffle(route.a2, size, [parts[0], *got], outs, points, nc, len(steps))
+    got = swap(parts[1:], [route.shift((0, gx, 0, gy)) for gx, gy in steps[1:]])
+    parts = shuffle(route.a3, size, [parts[0], *got], [bf16(k, points // nz)] * nz, points, len(steps), nz)
+    got = swap(parts[1:], [route.shift((d, 0, 0, 0)) for d in range(1, nz)])
+    return [parts[0], *got]
+
+
+def tile_of(size, parts, hot, tile_ref):
+    def block(i, carry):
+        at = pl.ds(pl.multiple_of(i * size, 16), size)
+        have = jnp.concatenate([r[at] for r in parts], axis=1)
+        tile_ref[at] = jnp.dot(have, hot[...], preferred_element_type=jnp.float32).astype(jnp.bfloat16)
+        return carry
+
+    lax.fori_loop(0, tile_ref.shape[0] // size, block, 0)
+
+
+def cells_hot(place, mask, hot):
+    lat_rows, lon_cells = mask.shape
+    index = lax.broadcasted_iota(jnp.int32, (hot.shape[0], lon_cells), 0)
+    for y in range(lat_rows):
+        chosen = (index == place[y : y + 1]) & (mask[y : y + 1] > 0)
+        hot[:, y * lon_cells : (y + 1) * lon_cells] = jnp.where(chosen, 1.0, 0.0).astype(jnp.bfloat16)
+
+
+def regroup_b_kernel(route, size, n_parts, capacity, *refs):
+    parts = refs[:n_parts]
+    ocean_ref, owner_ref, slot_ref, cell_ref, mask_ref, tile_ref, aux_ref, hot = refs[n_parts:]
+    mask = mask_ref[...]
+    cells_hot(route.b_end(cell_ref[...]), mask, hot)
+    k = tile_ref.shape[0]
+    tile_of(size, parts, hot, tile_ref)
+    lat_rows, lon_cells = mask.shape
+    owner = owner_ref[...]
+    z, x, c, _ = route.here()
+    za, xa, ca = owner // (route.nx * route.nc), owner // route.nc % route.nx, owner % route.nc
+    gz, gx = (z - za + route.nz) % route.nz, (x - xa + route.nx) % route.nx
+    gc = (c - ca + route.nc) % route.nc
+    deep = ocean_ref.shape[0]
+    spot = lax.broadcasted_iota(jnp.int32, (lat_rows, deep), 1)
+    at = gz * (2 * capacity) + slot_ref[...]
+    u = v = 0.0
+    for i in range(route.nc):
+        for j in range(route.nx):
+            lanes = slice(j * lon_cells, (j + 1) * lon_cells)
+            block = ocean_ref[:, lanes] if i == 0 else parts[i][k:, lanes]
+            here = (gc == i) & (gx == j)
+            u += jnp.dot(jnp.where((spot == at) & here, 1.0, 0.0).astype(jnp.bfloat16), block, preferred_element_type=jnp.float32)
+            v += jnp.dot(
+                jnp.where((spot == at + capacity) & here, 1.0, 0.0).astype(jnp.bfloat16), block, preferred_element_type=jnp.float32
+            )
+    aux_ref[0] = u
+    aux_ref[1] = v
+    aux_ref[2] = mask.astype(jnp.float32)
+
+
+def regroup_b(route, size, parts, ocean, owner, slot, cell, mask, capacity):
+    lat_rows, lon_cells = cell.shape
+    return pl.pallas_call(
+        functools.partial(regroup_b_kernel, route, size, len(parts), capacity),
+        out_shape=(bf16(parts[0].shape[0], route.points), jax.ShapeDtypeStruct((3, lat_rows, lon_cells), jnp.float32)),
+        in_specs=[VMEM] * (len(parts) + 5),
+        out_specs=(VMEM,) * 2,
+        scratch_shapes=hot_scratch(route.points),
+        name="regroup_b",
+        compiler_params=GRANT,
+    )(*parts, ocean, owner, slot, cell, mask)
+
+
+def pick_column(y_cells, x, lat_rows, lon_cells):
+    want = lax.broadcasted_iota(jnp.int32, (lat_rows, y_cells), 0) * lon_cells + x
+    return jnp.where(lax.broadcasted_iota(jnp.int32, (lat_rows, y_cells), 1) == want, 1.0, 0.0).astype(jnp.bfloat16)
+
+
+def regroup_a_kernel(route, size, n_parts, *refs):
+    parts = refs[:n_parts]
+    cell_ref, mask_ref, first_ref, aux_ref, tile_ref, row_ref, near_ref, far_ref, west_ref, hot = refs[n_parts:]
+    mask = mask_ref[...]
+    lat_rows, lon_cells = mask.shape
+    points = route.points
+    cells_hot(route.a_end(cell_ref[...]), mask, hot)
+    tile_of(size, parts, hot, tile_ref)
+    kb, ka = first_ref.shape[0], tile_ref.shape[0]
+    spectral = kb + ka
+    u, v, sea = aux_ref[0], aux_ref[1], aux_ref[2]
+    _, _, c, y = route.here()
+    facing = y == 0
+    last = (lat_rows - 1) * lon_cells
+    row_ref[:kb] = jnp.where(facing, first_ref[:, last : last + lon_cells], first_ref[:, :lon_cells])
+    row_ref[kb:spectral] = jnp.where(facing, tile_ref[:, last : last + lon_cells], tile_ref[:, :lon_cells])
+    low = jnp.concatenate([u[:1], v[:1], sea[:1], jnp.zeros((5, lon_cells), jnp.float32)], axis=0)
+    high = jnp.concatenate([u[-1:], v[-1:], sea[-1:], jnp.zeros((5, lon_cells), jnp.float32)], axis=0)
+    row_ref[spectral:] = jnp.where(facing, high, low).astype(jnp.bfloat16)
+    contract = (((1,), (1,)), ((), ()))
+    pad = near_ref.shape[1] - spectral
+    spot = lax.broadcasted_iota(jnp.int32, (lat_rows, pad), 1)
+    cols = []
+    for at in (0, lon_cells - 1):
+        pick = pick_column(points, at, lat_rows, lon_cells)
+        one = lax.dot_general(pick, first_ref[...], contract, preferred_element_type=jnp.float32)
+        two = lax.dot_general(pick, tile_ref[...], contract, preferred_element_type=jnp.float32)
+        extra = jnp.where(
+            spot == 0, u[:, at : at + 1], jnp.where(spot == 1, v[:, at : at + 1], jnp.where(spot == 2, sea[:, at : at + 1], 0.0))
+        )
+        cols.append(jnp.concatenate([one, two, extra], axis=1))
+    west, east = cols
+    near_ref[...] = jnp.where(c % 2 == 0, east, west).astype(jnp.bfloat16)
+    far_ref[...] = jnp.where(c % 2 == 0, west, east).astype(jnp.bfloat16)
+    west_ref[...] = west.astype(jnp.bfloat16)
+
+
+def regroup_a(route, size, parts, cell, mask, first, aux):
+    lat_rows, lon_cells = cell.shape
+    k = parts[0].shape[0]
+    spectral = k + first.shape[0]
+    wide = -(-(spectral + 3) // 128) * 128
+    edge = bf16(lat_rows, wide)
+    return pl.pallas_call(
+        functools.partial(regroup_a_kernel, route, size, len(parts)),
+        out_shape=(bf16(k, route.points), bf16(spectral + 8, lon_cells), edge, edge, edge),
+        in_specs=[VMEM] * (len(parts) + 4),
+        out_specs=(VMEM,) * 5,
+        scratch_shapes=hot_scratch(route.points),
+        name="regroup_a",
+        compiler_params=GRANT,
+    )(*parts, cell, mask, first, aux)
 
 
 def upwind(speed, here, there):
     return jnp.where(speed > 0.0, here, there) * speed
 
 
-def step_kernel(group_ref, tile_ref, south_ref, north_ref, west_ref, east_ref, cols_ref, aux_ref, trig_ref, freq_ref, out_ref, halo, turns, lay):
-    spectral = tile_ref.shape[0]
+def step_kernel(route, n_tiles, group_ref, *refs):
+    tiles = refs[:n_tiles]
+    south_ref, north_ref, west_ref, east_ref, own_ref, aux_ref, trig_ref, freq_ref, out_ref, halo, turns, lay = refs[n_tiles:]
+    spectral = sum(t.shape[0] for t in tiles)
     rows, lanes = turns.shape[1], aux_ref.shape[2]
     lat_rows = aux_ref.shape[1]
     dirs = rows // 2
     f32 = jnp.float32
     u, v, sea = aux_ref[0], aux_ref[1], aux_ref[2]
     lane = lax.broadcasted_iota(jnp.int32, (lat_rows, lanes), 1)
-    west = west_ref[...].astype(f32)
-    east = east_ref[...].astype(f32)
+    below = south_ref[spectral : spectral + 8].astype(f32)
+    above = north_ref[spectral : spectral + 8].astype(f32)
+    west_b, east_b = west_ref[...], east_ref[...]
+    if route:
+        _, _, c, y = route.here()
+        below = jnp.where(y == 1, below, 0.0)
+        above = jnp.where(y == 0, above, 0.0)
+        west_b, east_b = jnp.where(c % 2 == 0, east_b, west_b), jnp.where(c % 2 == 0, west_b, east_b)
+    west, east = west_b.astype(f32), east_b.astype(f32)
 
     def sides(a, i):
         at = spectral + i
@@ -149,8 +566,6 @@
     _, me = sides(sea, 2)
     open_x = sea * me
     face_u = 0.5 * (u + ue)
-    below = south_ref[spectral : spectral + 8].astype(f32)
-    above = north_ref[spectral : spectral + 8].astype(f32)
     ut = jnp.concatenate([below[0:1], u, above[0:1]], axis=0)
     vt = jnp.concatenate([below[1:2], v, above[1:2]], axis=0)
     mt = jnp.concatenate([below[2:3], sea, above[2:3]], axis=0)
@@ -164,7 +579,7 @@
     for y in range(lat_rows):
         sl = slice(y, y + 1)
         turns[y] = turn_scale * (fs * fc * (ux[sl] - vy[sl]) + fs * fs * uy[sl] - fc * fc * vx[sl])
-    own = cols_ref[0, :, :spectral].astype(f32)
+    own = own_ref[:, :spectral].astype(f32)
     wide_u = west[:, spectral : spectral + 1]
     speed = freq_ref[0:1] + 0.5 * (wide_u + u[:, 0:1])
     flux_w = (west[:, spectral + 2 : spectral + 3] * sea[:, 0:1]) * upwind(speed, west[:, :spectral], own)
@@ -172,7 +587,7 @@
     rest = flux_w - hi.astype(f32)
     mid = rest.astype(jnp.bfloat16)
     low = (rest - mid.astype(f32)).astype(jnp.bfloat16)
-    left = jnp.concatenate([hi, mid, low, east_ref[:, :spectral]], axis=0)
+    left = jnp.concatenate([hi, mid, low, east_b[:, :spectral]], axis=0)
     total = lat_rows * lanes
     j = lax.broadcasted_iota(jnp.int32, (4 * lat_rows, total), 0)
     c = lax.broadcasted_iota(jnp.int32, (4 * lat_rows, total), 1)
@@ -188,13 +603,15 @@
     seam_down = (row == 0) | (row == dirs)
     cosd, sind = trig_ref[:, 0:1], trig_ref[:, 1:2]
 
-    def pair(i, carry):
-        at = pl.multiple_of(i * rows, 8)
+    def pair(tile_ref, start, i, carry):
+        mine = pl.ds(pl.multiple_of(i * rows, 8), rows)
+        at = pl.multiple_of(start + i * rows, 8)
         sl = pl.ds(at, rows)
-        speed_f = jnp.where(top, group_ref[2 * i], group_ref[2 * i + 1])
+        f = start // dirs + 2 * i
+        speed_f = jnp.where(top, group_ref[f], group_ref[f + 1])
         gc = speed_f * cosd
         gs = speed_f * sind
-        value = [tile_ref[sl, y * lanes : (y + 1) * lanes].astype(f32) for y in range(lat_rows)]
+        value = [tile_ref[mine, y * lanes : (y + 1) * lanes].astype(f32) for y in range(lat_rows)]
         below_v = south_ref[sl, :].astype(f32)
         above_v = north_ref[sl, :].astype(f32)
         flux_s = None
@@ -220,19 +637,22 @@
         out_ref[pl.ds(pl.multiple_of(at * lat_rows, 8), rows * lat_rows), :] = lay[...].astype(jnp.bfloat16)
         return carry
 
-    lax.fori_loop(0, spectral // rows, pair, 0)
-
-
-def step(tab, tile, south, north, west, east, cols, aux):
-    spectral, points = tile.shape
+    start = 0
+    for t in tiles:
+        lax.fori_loop(0, t.shape[0] // rows, functools.partial(pair, t, start), 0)
+        start += t.shape[0]
+
+
+def step(tab, route, tiles, south, north, west, east, own, aux):
     freqs, dirs = tab["group"].shape[0], tab["cosd"].shape[0]
+    spectral, points = freqs * dirs, tiles[0].shape[1]
     _, lat_rows, lon_cells = aux.shape
     trig = np.tile(np.stack([tab["cosd"], tab["sind"], tab["fcos"], tab["fsin"]], axis=1), (2, 1))
     freq = np.outer(tab["group"], tab["cosd"]).reshape(1, spectral)
     return pl.pallas_call(
-        step_kernel,
+        functools.partial(step_kernel, route, len(tiles)),
         out_shape=jax.ShapeDtypeStruct((spectral * lat_rows, lon_cells), jnp.bfloat16),
-        in_specs=[SMEM] + [VMEM] * 9,
+        in_specs=[SMEM] + [VMEM] * (len(tiles) + 8),
         out_specs=VMEM,
         scratch_shapes=[
             pltpu.VMEM((spectral, points), jnp.float32),
@@ -240,10 +660,21 @@
             pltpu.VMEM((2 * dirs * lat_rows, lon_cells), jnp.float32),
         ],
         name="step",
-    )(tab["group"], tile, south, north, west, east, cols, aux, trig, freq)
-
-
-def body(spec_pts, wind_u, wind_v, ocean_current, block_owner, block_slot, cell_source, land_mask):
+        compiler_params=GRANT,
+    )(tab["group"], *tiles, south, north, west, east, own, aux, trig, freq)
+
+
+def lon_grid(mesh):
+    spots = [(d.coords[2], d.coords[0], d.core_on_chip) for d in mesh.devices[:, 0] if hasattr(d, "coords")]
+    if len(spots) != mesh.shape["lon"]:
+        return None
+    sizes = tuple(len({s[i] for s in spots}) for i in range(3))
+    base = [min(s[i] for s in spots) for i in range(3)]
+    flat = [((s[0] - base[0]) * sizes[1] + s[1] - base[1]) * sizes[2] + s[2] - base[2] for s in spots]
+    return sizes if flat == list(range(len(spots))) else None
+
+
+def body(grid, spec_pts, wind_u, wind_v, ocean_current, block_owner, block_slot, cell_source, land_mask):
     freqs, dirs, points = spec_pts.shape
     lat_rows, lon_cells = cell_source.shape
     n_lon, n_lat = lax.axis_size("lon"), lax.axis_size("lat")
@@ -251,8 +682,25 @@
     capacity = ocean_current.shape[2]
     spectral = freqs * dirs
     tab = tables(freqs, dirs)
+    if staged(grid, n_lat):
+        route = Route(grid, n_lat, per_dest)
+        count = -(-freqs * 5 // 9) // 4 * 4
+        size = 4 * dirs
+        ocean = ocean_current.reshape(2 * capacity, lon_cells)
+        *parts, base = source_b(tab, route, 0, count, spec_pts, wind_u, wind_v, ocean)
+        parts_a = source_a(tab, route, count, freqs - count, spec_pts, wind_u, wind_v, base)
+        parts, ocean = exchange_b(route, size, parts, ocean)
+        parts_a = exchange_a(route, size, parts_a)
+        tile_b, aux = regroup_b(route, size, parts, ocean, block_owner, block_slot, cell_source, land_mask, capacity)
+        tile_a, row, near, far, own = regroup_a(route, size, parts_a, cell_source, land_mask, tile_b, aux)
+        ring = [(i, (i - 1) % n_lon if i % 2 == 0 else (i + 1) % n_lon) for i in range(n_lon)]
+        chip = [(i, i ^ 1) for i in range(n_lon)]
+        row = lax.ppermute(row, "lat", [(0, 1), (1, 0)])
+        far = lax.ppermute(far, "lon", ring)
+        near = lax.ppermute(near, "lon", chip)
+        out = step(tab, route, [tile_b, tile_a], row, row, near, far, own, aux)
+        return out.reshape(freqs, dirs, lat_rows, lon_cells)
     everyone = ("lon", "lat")
-
     want = block_owner * capacity + block_slot
     ocean = lax.all_gather(ocean_current[:, 0], "lon", axis=1, tiled=True)
     sourced = source(tab, spec_pts, wind_u, wind_v)
@@ -271,13 +719,22 @@
     down = [(j, i) for i, j in up]
     south = lax.ppermute(rows[1], "lat", up)
     north = lax.ppermute(rows[0], "lat", down)
-    out = step(tab, tile, south, north, west, east, cols, aux)
+    out = step(tab, None, [tile], south, north, west, east, cols[0], aux)
     return out.reshape(freqs, dirs, lat_rows, lon_cells)
 
 
+def staged(grid, n_lat):
+    return bool(grid) and n_lat == 2 and grid[2] == 2
+
+
 def solution(mesh):
+    grid = lon_grid(mesh)
+
+    def layer(*args):
+        return body(grid, *args)
+
     return jax.shard_map(
-        body,
+        layer,
         mesh=mesh,
         in_specs=(
             P(None, None, ("lon", "lat")),

time: 91 us -> 91.8 us (level)
  blocking collectives: 40.3 us -> 0 us
  waiting for transfers between devices: 5.81 us -> 37.3 us
  starting transfers between devices: 19.1 us -> 27.4 us
  Pallas kernels: 15.8 us -> 20.2 us
  local copies, waits for them, and re-layouts: 8.25 us -> 5.72 us
  other arithmetic: 1.21 us -> 0 us
    all_gather x1 -> x0, blocking collectives: 40.3 us -> none  [body(): ocean = lax.all_gather(ocean_current[:, 0], 'lon', axis=1, tiled=True)]
    ppermute x4 -> x17, waiting for transfers between devices: 5.81 us -> 37.3 us  [the longest x14 33.6 us: swap(): moved.append(lax.ppermute(part, ('lon', 'lat'), perm))]
    ppermute x4 -> x17, starting transfers between devices: 11.8 us -> 27.4 us  [the longest x14 21.4 us: swap(): moved.append(lax.ppermute(part, ('lon', 'lat'), perm))]
    all_to_all x1 -> x0, starting transfers between devices: 7.33 us -> none  [body(): lax.all_to_all(packed, everyone, split_axis=0, concat_axis=0, tiled=True)]
    pallas_call x3 -> x9, Pallas kernels: 15.8 us -> 20.2 us  [the longest x1 7.02 us: step(): pl.pallas_call(functools.partial(step_kernel, route, len(tiles)), out_sha...]
    unnamed x19 -> x40, local copies, waits for them, and re-layouts: 2.04 us -> 5.72 us
    reshape x2 -> x0, local copies, waits for them, and re-layouts: 3.04 us -> none  [body(): sourced.reshape(spectral, points)]
    squeeze x2 -> x0, local copies, waits for them, and re-layouts: 1.85 us -> none  [the longest x1 1.12 us: body(): north = lax.ppermute(rows[0], 'lat', down)]
  transfers between devices with their start and end apart: 5 -> 17, of which waited for: 2 -> 10; matrix products, arithmetic and copies ran while one was open for 2% -> 0% of each run, Pallas kernels for 0% -> 8%
where the time goes in v2:
time: 91.8 us; the launch traced here: 90.8 us
  waiting for transfers between devices  37.3 us (41%)
  starting transfers between devices  27.4 us (30%)
  Pallas kernels  20.2 us (22%)
  local copies, waits for them, and re-layouts  5.72 us (6%)
    ppermute x14, waiting for transfers between devices, swap(): moved.append(lax.ppermute(part, ('lon', 'lat'), perm))  33.6 us
    ppermute x14, starting transfers between devices, swap(): moved.append(lax.ppermute(part, ('lon', 'lat'), perm))  21.4 us
    pallas_call x1, Pallas kernels, step(): pl.pallas_call(functools.partial(step_kernel, route, len(tiles)), out_sha...  7.02 us
    unnamed x40, local copies, waits for them, and re-layouts  5.72 us
    pallas_call x4, Pallas kernels, shuffle(): pl.pallas_call(functools.partial(shuffle_body, index, size, n_in, len(ins...  4.92 us
    ppermute x1, starting transfers between devices, body(): far = lax.ppermute(far, 'lon', ring)  4.45 us
    pallas_call x1, Pallas kernels, source_b(): pl.pallas_call(kernel, out_shape=(*outs, jax.ShapeDtypeStruct((1, points)...  2.56 us
    ppermute x1, waiting for transfers between devices, body(): row = lax.ppermute(row, 'lat', [(0, 1), (1, 0)])  2.31 us
  transfers between devices with their start and end apart: 17, of which 10 were waited for; matrix products, arithmetic and copies ran while one was open for 0% of the time, Pallas kernels for 8%

profile of v2, /device:TPU:0, one launch (start us, length us, event | category | flops | bytes accessed | tf_op | source)
XLA Modules:
  0.0 90.8 jit_solution(1671047181924623125)
XLA Ops:
  0.0 1.4 %copy-done = bf16[36,36,512]{2,1,0:T(8,128)(2,1)S(1)} copy-done((bf16[36,36,512]{2,1,0:T(8,128)(2,1)S(1)}, bf16[36,36,512]{2,1,0:T(8,128)(2,1)}, u32[]{:S(2)}) %copy-start) | copy-done | bytes 1327128
  1.4 0.7 copy-done.2
  2.1 0.7 copy-done.5
  2.8 0.7 copy-done.7
  3.5 0.7 copy-done.9
  4.2 0.7 copy-done.14
  4.8 0.7 copy-done.15
  5.5 2.6 %source_b.1 = (bf16[720,128]{1,0:T(8,128)(2,1)S(1)}, bf16[736,128]{1,0:T(8,128)(2,1)S(1)}, bf16[736,128]{1,0:T(8,128)(2,1)S(1)}, bf16[736,128]{1,0:T(8,128)(2,1)S(1)}, f32[1,512]{1,0:T(1,128)S(1)}) custom-call(f32[36]{0:T(128)S(1)} %copy-done.15, f32[36]{0:T(128)S(1)} %copy-done.14, bf16[36,36,512]{2,1,0:T(8,128)(2,1)S(1)} %copy-done, f32[1,512]{1,0:T(1,128)S(1)} %bitcast.6, ...), custom_call_target="tpu_custom_call" | custom-call | tf_op jit(solution)/shard_map/source_b/pallas_call | solution.py:300
  8.1 3.1 %collective-permute-start = (bf16[736,128]{1,0:T(8,128)(2,1)S(1)}, bf16[736,128]{1,0:T(8,128)(2,1)S(1)}, u32[]{:S(2)}, u32[]{:S(2)}) collective-permute-start(bf16[736,128]{1,0:T(8,128)(2,1)S(1)} %get-tuple-element.36), channel_id=1, source_target_pairs={{0,8},{1,9},{2,10},{3,11},{4,12},{5,13},{6,14},{7,15},{8,16},{9,17... | collective-permute-start | bytes 565256 | tf_op jit(solution)/shard_map/ppermute | solution.py:359
  11.2 2.6 %collective-permute-start.1 = (bf16[736,128]{1,0:T(8,128)(2,1)S(1)}, bf16[736,128]{1,0:T(8,128)(2,1)S(1)}, u32[]{:S(2)}, u32[]{:S(2)}) collective-permute-start(bf16[736,128]{1,0:T(8,128)(2,1)S(1)} %get-tuple-element.37), channel_id=1, source_target_pairs={{0,16},{1,17},{2,18},{3,19},{4,20},{5,21},{6,22},{7,23},{8,24},{9,... | collective-permute-start | bytes 565256 | tf_op jit(solution)/shard_map/ppermute | solution.py:359
  13.8 1.4 %collective-permute-start.2 = (bf16[736,128]{1,0:T(8,128)(2,1)S(1)}, bf16[736,128]{1,0:T(8,128)(2,1)S(1)}, u32[]{:S(2)}, u32[]{:S(2)}) collective-permute-start(bf16[736,128]{1,0:T(8,128)(2,1)S(1)} %get-tuple-element.38), channel_id=1, source_target_pairs={{0,24},{1,25},{2,26},{3,27},{4,28},{5,29},{6,30},{7,31},{8,0},{9,1... | collective-permute-start | bytes 565256 | tf_op jit(solution)/shard_map/ppermute | solution.py:359
  15.1 3.8 %collective-permute-done.refs_1_ = bf16[736,128]{1,0:T(8,128)(2,1)S(1)} collective-permute-done((bf16[736,128]{1,0:T(8,128)(2,1)S(1)}, bf16[736,128]{1,0:T(8,128)(2,1)S(1)}, u32[]{:S(2)}, u32[]{:S(2)}) %collective-permute-start) | collective-permute-done | bytes 188448 | tf_op jit(solution)/shard_map/ppermute | solution.py:359
  18.9 7.2 %collective-permute-done.1.refs_2_ = bf16[736,128]{1,0:T(8,128)(2,1)S(1)} collective-permute-done((bf16[736,128]{1,0:T(8,128)(2,1)S(1)}, bf16[736,128]{1,0:T(8,128)(2,1)S(1)}, u32[]{:S(2)}, u32[]{:S(2)}) %collective-permute-start.1) | collective-permute-done | bytes 188448 | tf_op jit(solution)/shard_map/ppermute | solution.py:359
  26.1 1.4 %shard_map.145 = (bf16[720,128]{1,0:T(8,128)(2,1)S(1)}, bf16[720,128]{1,0:T(8,128)(2,1)S(1)}, bf16[784,128]{1,0:T(8,128)(2,1)S(1)}, bf16[720,128]{1,0:T(8,128)(2,1)S(1)}, bf16[64,128]{1,0:T(8,128)(2,1)S(1)}) custom-call(bf16[720,128]{1,0:T(8,128)(2,1)S(1)} %get-tuple-element.35.refs_0_, bf16[736,128]{1,0:T(8,128)(2,1)S(1)} %collective-permute-done.refs_1_, ...), custom_call_target="tpu_custom_call" | custom-call | tf_op jit(solution)/shard_map/pallas_call | solution.py:326
  27.5 1.6 %collective-permute-start.4 = (bf16[784,128]{1,0:T(8,128)(2,1)S(1)}, bf16[784,128]{1,0:T(8,128)(2,1)S(1)}, u32[]{:S(2)}, u32[]{:S(2)}) collective-permute-start(bf16[784,128]{1,0:T(8,128)(2,1)S(1)} %get-tuple-element.41), channel_id=1, source_target_pairs={{0,4},{1,5},{2,6},{3,7},{4,0},{5,1},{6,2},{7,3},{8,12},{9,13},{10,... | collective-permute-start | bytes 602120 | tf_op jit(solution)/shard_map/ppermute | solution.py:359
  29.0 0.0 copy-start.18
  29.1 2.1 %source_a.1 = (bf16[576,256]{1,0:T(8,128)(2,1)S(1)}, bf16[576,256]{1,0:T(8,128)(2,1)S(1)}) custom-call(f32[36]{0:T(128)S(1)} %copy-done.15, f32[36]{0:T(128)S(1)} %copy-done.14, bf16[36,36,512]{2,1,0:T(8,128)(2,1)S(1)} %copy-done.1, f32[1,512]{1,0:T(1,128)S(1)} %bitcast.7, f32[1,512]{1,0:T(1,128)S(1)} %bitcast.9, f32[36,2]{1,0:T(8,128)S(1)} %copy-done.3, ...), custom_call_target="tpu_custom_call" | custom-call | tf_op jit(solution)/shard_map/source_a/pallas_call | solution.py:314
  31.2 0.1 collective-permute-start.7
  31.2 1.6 %collective-permute-start.3 = (bf16[720,128]{1,0:T(8,128)(2,1)S(1)}, bf16[720,128]{1,0:T(8,128)(2,1)S(1)}, u32[]{:S(2)}, u32[]{:S(2)}) collective-permute-start(bf16[720,128]{1,0:T(8,128)(2,1)S(1)} %get-tuple-element.40), channel_id=1, source_target_pairs={{0,1},{1,0},{2,3},{3,2},{4,5},{5,4},{6,7},{7,6},{8,9},{9,8},{10,11... | collective-permute-start | bytes 552968 | tf_op jit(solution)/shard_map/ppermute | solution.py:359
  32.8 0.5 collective-permute-start.5
  33.3 8.9 %collective-permute-done.3.refs_1_ = bf16[720,128]{1,0:T(8,128)(2,1)S(1)} collective-permute-done((bf16[720,128]{1,0:T(8,128)(2,1)S(1)}, bf16[720,128]{1,0:T(8,128)(2,1)S(1)}, u32[]{:S(2)}, u32[]{:S(2)}) %collective-permute-start.3) | collective-permute-done | bytes 184352 | tf_op jit(solution)/shard_map/ppermute | solution.py:359
  42.2 1.3 %shard_map.146 = (bf16[720,256]{1,0:T(8,128)(2,1)S(1)}, bf16[784,256]{1,0:T(8,128)(2,1)S(1)}, bf16[64,256]{1,0:T(8,128)(2,1)S(1)}) custom-call(bf16[720,128]{1,0:T(8,128)(2,1)S(1)} %get-tuple-element.39.refs_0_, bf16[720,128]{1,0:T(8,128)(2,1)S(1)} %collective-permute-done.3.refs_1_, bf16[784,128]{1,0:T(8,128)(2,1)S(1)} %collective-permute-done.4.refs_2_, ...), custom_call_target="tpu_custom_call" | custom-call | tf_op jit(solution)/shard_map/pallas_call | solution.py:326
  43.6 0.1 collective-permute-start.6
  43.7 1.1 %shard_map.147 = (bf16[576,128]{1,0:T(8,128)(2,1)S(1)}, bf16[576,128]{1,0:T(8,128)(2,1)S(1)}, bf16[576,128]{1,0:T(8,128)(2,1)S(1)}, bf16[576,128]{1,0:T(8,128)(2,1)S(1)}) custom-call(bf16[576,256]{1,0:T(8,128)(2,1)S(1)} %get-tuple-element.49.refs_0_, bf16[576,256]{1,0:T(8,128)(2,1)S(1)} %collective-permute-done.7.refs_1_), custom_call_target="tpu_custom_call" | custom-call | tf_op jit(solution)/shard_map/pallas_call | solution.py:326
  44.8 0.0 copy-start.4
  44.8 0.0 copy-start.13
  44.8 0.0 copy-start.16
  44.8 1.6 %collective-permute-start.8 = (bf16[576,128]{1,0:T(8,128)(2,1)S(1)}, bf16[576,128]{1,0:T(8,128)(2,1)S(1)}, u32[]{:S(2)}, u32[]{:S(2)}) collective-permute-start(bf16[576,128]{1,0:T(8,128)(2,1)S(1)} %get-tuple-element.52), channel_id=1, source_target_pairs={{0,1},{1,0},{2,3},{3,2},{4,5},{5,4},{6,7},{7,6},{8,9},{9,8},{10,11... | collective-permute-start | bytes 442376 | tf_op jit(solution)/shard_map/ppermute | solution.py:359
  46.4 0.5 collective-permute-start.9
  47.0 1.4 %collective-permute-start.10 = (bf16[576,128]{1,0:T(8,128)(2,1)S(1)}, bf16[576,128]{1,0:T(8,128)(2,1)S(1)}, u32[]{:S(2)}, u32[]{:S(2)}) collective-permute-start(bf16[576,128]{1,0:T(8,128)(2,1)S(1)} %get-tuple-element.54), channel_id=1, source_target_pairs={{0,5},{1,4},{2,7},{3,6},{4,1},{5,0},{6,3},{7,2},{8,13},{9,12},{10,... | collective-permute-start | bytes 442376 | tf_op jit(solution)/shard_map/ppermute | solution.py:359
  48.4 2.8 %collective-permute-done.8.refs_1_ = bf16[576,128]{1,0:T(8,128)(2,1)S(1)} collective-permute-done((bf16[576,128]{1,0:T(8,128)(2,1)S(1)}, bf16[576,128]{1,0:T(8,128)(2,1)S(1)}, u32[]{:S(2)}, u32[]{:S(2)}) %collective-permute-start.8) | collective-permute-done | bytes 147488 | tf_op jit(solution)/shard_map/ppermute | solution.py:359
  51.2 2.0 %collective-permute-done.9.refs_2_ = bf16[576,128]{1,0:T(8,128)(2,1)S(1)} collective-permute-done((bf16[576,128]{1,0:T(8,128)(2,1)S(1)}, bf16[576,128]{1,0:T(8,128)(2,1)S(1)}, u32[]{:S(2)}, u32[]{:S(2)}) %collective-permute-start.9) | collective-permute-done | bytes 147488 | tf_op jit(solution)/shard_map/ppermute | solution.py:359
  53.2 2.3 %collective-permute-done.10.refs_3_ = bf16[576,128]{1,0:T(8,128)(2,1)S(1)} collective-permute-done((bf16[576,128]{1,0:T(8,128)(2,1)S(1)}, bf16[576,128]{1,0:T(8,128)(2,1)S(1)}, u32[]{:S(2)}, u32[]{:S(2)}) %collective-permute-start.10) | collective-permute-done | bytes 147488 | tf_op jit(solution)/shard_map/ppermute | solution.py:359
  55.5 1.1 %shard_map.148 = (bf16[576,128]{1,0:T(8,128)(2,1)S(1)}, bf16[576,128]{1,0:T(8,128)(2,1)S(1)}, bf16[576,128]{1,0:T(8,128)(2,1)S(1)}, bf16[576,128]{1,0:T(8,128)(2,1)S(1)}) custom-call(bf16[576,128]{1,0:T(8,128)(2,1)S(1)} %get-tuple-element.51.refs_0_, bf16[576,128]{1,0:T(8,128)(2,1)S(1)} %collective-permute-done.8.refs_1_, ...), custom_call_target="tpu_custom_call" | custom-call | tf_op jit(solution)/shard_map/pallas_call | solution.py:326
  56.6 4.6 %collective-permute-start.11 = (bf16[576,128]{1,0:T(8,128)(2,1)S(1)}, bf16[576,128]{1,0:T(8,128)(2,1)S(1)}, u32[]{:S(2)}, u32[]{:S(2)}) collective-permute-start(bf16[576,128]{1,0:T(8,128)(2,1)S(1)} %get-tuple-element.56), channel_id=1, source_target_pairs={{0,8},{1,9},{2,10},{3,11},{4,12},{5,13},{6,14},{7,15},{8,16},{9,17... | collective-permute-start | bytes 442376 | tf_op jit(solution)/shard_map/ppermute | solution.py:359
  61.2 1.6 %collective-permute-start.12 = (bf16[576,128]{1,0:T(8,128)(2,1)S(1)}, bf16[576,128]{1,0:T(8,128)(2,1)S(1)}, u32[]{:S(2)}, u32[]{:S(2)}) collective-permute-start(bf16[576,128]{1,0:T(8,128)(2,1)S(1)} %get-tuple-element.57), channel_id=1, source_target_pairs={{0,16},{1,17},{2,18},{3,19},{4,20},{5,21},{6,22},{7,23},{8,24},{9,... | collective-permute-start | bytes 442376 | tf_op jit(solution)/shard_map/ppermute | solution.py:359
  62.8 0.8 collective-permute-start.13
  63.6 0.1 copy.16.refs_3_
  63.7 0.1 copy.17.refs_4_
  63.8 1.6 %regroup_b.1 = (bf16[720,512]{1,0:T(8,128)(2,1)S(1)}, f32[3,4,128]{2,1,0:T(4,128)S(1)}) custom-call(bf16[720,256]{1,0:T(8,128)(2,1)S(1)} %get-tuple-element.44.refs_0_, bf16[784,256]{1,0:T(8,128)(2,1)S(1)} %collective-permute-done.6.refs_1_, bf16[64,256]{1,0:T(8,128)(2,1)S(1)} %get-tuple-element.46.refs_2_, s32[4,1]{1,0:T(4,128)S(1)} %copy.16.refs_3_, ...), custom_call_target="tpu_custom_call" | custom-call | tf_op jit(solution)/shard_map/regroup_b/pallas_call | solution.py:464
  65.4 1.6 %collective-permute-done.11.refs_1_ = bf16[576,128]{1,0:T(8,128)(2,1)S(1)} collective-permute-done((bf16[576,128]{1,0:T(8,128)(2,1)S(1)}, bf16[576,128]{1,0:T(8,128)(2,1)S(1)}, u32[]{:S(2)}, u32[]{:S(2)}) %collective-permute-start.11) | collective-permute-done | bytes 147488 | tf_op jit(solution)/shard_map/ppermute | solution.py:359
  67.0 5.0 %collective-permute-done.12.refs_2_ = bf16[576,128]{1,0:T(8,128)(2,1)S(1)} collective-permute-done((bf16[576,128]{1,0:T(8,128)(2,1)S(1)}, bf16[576,128]{1,0:T(8,128)(2,1)S(1)}, u32[]{:S(2)}, u32[]{:S(2)}) %collective-permute-start.12) | collective-permute-done | bytes 147488 | tf_op jit(solution)/shard_map/ppermute | solution.py:359
  72.0 2.0 %regroup_a.1 = (bf16[576,512]{1,0:T(8,128)(2,1)S(1)}, bf16[1304,128]{1,0:T(8,128)(2,1)S(1)}, bf16[4,1408]{1,0:T(4,128)(2,1)S(1)}, bf16[4,1408]{1,0:T(4,128)(2,1)S(1)}, bf16[4,1408]{1,0:T(4,128)(2,1)S(1)}) custom-call(bf16[576,128]{1,0:T(8,128)(2,1)S(1)} %get-tuple-element.55.refs_0_, bf16[576,128]{1,0:T(8,128)(2,1)S(1)} %collective-permute-done.11.refs_1_, ...), custom_call_target="tpu_custom_call" | custom-call | tf_op jit(solution)/shard_map/regroup_a/pallas_call | solution.py:523
  74.0 1.6 %collective-permute-start.14 = (bf16[1304,128]{1,0:T(8,128)(2,1)S(1)}, bf16[1304,128]{1,0:T(8,128)(2,1)S(1)}, u32[]{:S(2)}, u32[]{:S(2)}) collective-permute-start(bf16[1304,128]{1,0:T(8,128)(2,1)S(1)} %get-tuple-element.61), channel_id=1, source_target_pairs={{0,1},{1,0},{2,3},{3,2},{4,5},{5,4},{6,7},{7,6},{8,9},{9,8},{10,11... | collective-permute-start | bytes 1001480 | tf_op jit(solution)/shard_map/ppermute | solution.py:698
  75.6 4.4 %collective-permute-start.16 = (bf16[4,1408]{1,0:T(4,128)(2,1)S(1)}, bf16[4,1408]{1,0:T(4,128)(2,1)S(1)}, u32[]{:S(2)}, u32[]{:S(2)}) collective-permute-start(bf16[4,1408]{1,0:T(4,128)(2,1)S(1)} %get-tuple-element.63), channel_id=1, source_target_pairs={{0,30},{2,4},{4,2},{6,8},{8,6},{10,12},{12,10},{14,16},{16,14},{18... | collective-permute-start | bytes 33800 | tf_op jit(solution)/shard_map/ppermute | solution.py:699
  80.1 1.4 %collective-permute-done.16.refs_5_ = bf16[4,1408]{1,0:T(4,128)(2,1)S(1)} collective-permute-done((bf16[4,1408]{1,0:T(4,128)(2,1)S(1)}, bf16[4,1408]{1,0:T(4,128)(2,1)S(1)}, u32[]{:S(2)}, u32[]{:S(2)}) %collective-permute-start.16) | collective-permute-done | bytes 11296 | tf_op jit(solution)/shard_map/ppermute | solution.py:699
  81.5 2.3 %collective-permute-done.14.refs_2_.refs_3_ = bf16[1304,128]{1,0:T(8,128)(2,1)S(1)} collective-permute-done((bf16[1304,128]{1,0:T(8,128)(2,1)S(1)}, bf16[1304,128]{1,0:T(8,128)(2,1)S(1)}, u32[]{:S(2)}, u32[]{:S(2)}) %collective-permute-start.14) | collective-permute-done | bytes 333856 | tf_op jit(solution)/shard_map/ppermute | solution.py:698
  83.8 7.0 %step.1 = bf16[5184,128]{1,0:T(8,128)(2,1)} custom-call(f32[36]{0:T(128)S(1)} %copy-done.16, bf16[720,512]{1,0:T(8,128)(2,1)S(1)} %get-tuple-element.47.refs_6_.refs_0_, bf16[576,512]{1,0:T(8,128)(2,1)S(1)} %get-tuple-element.60.refs_1_, bf16[1304,128]{1,0:T(8,128)(2,1)S(1)} %collective-permute-done.14.refs_2_.refs_3_, ...), custom_call_target="tpu_custom_call" | custom-call | tf_op jit(solution)/shard_map/step/pallas_call | solution.py:652
  (35 shorter events, 0.1 us)
Async XLA Ops:
  0.0 26.1 %copy-start.6 = (bf16[2,1,8,128]{3,2,1,0:T(8,128)(2,1)S(1)}, bf16[2,1,8,128]{3,2,1,0:T(8,128)(2,1)}, u32[]{:S(2)}) copy-start(bf16[2,1,8,128]{3,2,1,0:T(8,128)(2,1)} %param.18) | copy-start | bytes 12292
  0.0 1.4 %copy-start = (bf16[36,36,512]{2,1,0:T(8,128)(2,1)S(1)}, bf16[36,36,512]{2,1,0:T(8,128)(2,1)}, u32[]{:S(2)}) copy-start(bf16[36,36,512]{2,1,0:T(8,128)(2,1)} %spec_ref.3) | copy-start | bytes 3981316
  1.4 0.7 copy-start.2
  2.1 0.7 copy-start.5
  2.8 0.7 copy-start.7
  3.5 0.7 copy-start.9
  4.2 0.7 copy-start.14
  4.8 0.7 copy-start.15
  5.5 23.5 %copy-start.1 = (bf16[36,36,512]{2,1,0:T(8,128)(2,1)S(1)}, bf16[36,36,512]{2,1,0:T(8,128)(2,1)}, u32[]{:S(2)}) copy-start(bf16[36,36,512]{2,1,0:T(8,128)(2,1)} %spec_ref.3) | copy-start | bytes 3981316
  5.5 23.5 %copy-start.3 = (f32[36,2]{1,0:T(8,128)S(1)}, f32[36,2]{1,0:T(8,128)}, u32[]{:S(2)}) copy-start(f32[36,2]{1,0:T(8,128)} %constant.14.clone.trig_ref) | copy-start | bytes 868
  5.5 23.5 %copy-start.8 = (f32[512]{0:T(512)S(1)}, f32[512]{0:T(512)}, u32[]{:S(2)}) copy-start(f32[512]{0:T(512)} %param.16) | copy-start | bytes 6148
  5.5 23.5 %copy-start.10 = (f32[512]{0:T(512)S(1)}, f32[512]{0:T(512)}, u32[]{:S(2)}) copy-start(f32[512]{0:T(512)} %param.17) | copy-start | bytes 6148
  8.1 10.8 %collective-permute-start = (bf16[736,128]{1,0:T(8,128)(2,1)S(1)}, bf16[736,128]{1,0:T(8,128)(2,1)S(1)}, u32[]{:S(2)}, u32[]{:S(2)}) collective-permute-start(bf16[736,128]{1,0:T(8,128)(2,1)S(1)} %get-tuple-element.36), channel_id=1, source_target_pairs={{0,8},{1,9},{2,10},{3,11},{4,12},{5,13},{6,14},{7,15},{8,16},{9,17... | collective-permute-start | bytes 565256 | tf_op jit(solution)/shard_map/ppermute | solution.py:359
  11.2 14.9 %collective-permute-start.1 = (bf16[736,128]{1,0:T(8,128)(2,1)S(1)}, bf16[736,128]{1,0:T(8,128)(2,1)S(1)}, u32[]{:S(2)}, u32[]{:S(2)}) collective-permute-start(bf16[736,128]{1,0:T(8,128)(2,1)S(1)} %get-tuple-element.37), channel_id=1, source_target_pairs={{0,16},{1,17},{2,18},{3,19},{4,20},{5,21},{6,22},{7,23},{8,24},{9,... | collective-permute-start | bytes 565256 | tf_op jit(solution)/shard_map/ppermute | solution.py:359
  13.8 12.3 %collective-permute-start.2 = (bf16[736,128]{1,0:T(8,128)(2,1)S(1)}, bf16[736,128]{1,0:T(8,128)(2,1)S(1)}, u32[]{:S(2)}, u32[]{:S(2)}) collective-permute-start(bf16[736,128]{1,0:T(8,128)(2,1)S(1)} %get-tuple-element.38), channel_id=1, source_target_pairs={{0,24},{1,25},{2,26},{3,27},{4,28},{5,29},{6,30},{7,31},{8,0},{9,1... | collective-permute-start | bytes 565256 | tf_op jit(solution)/shard_map/ppermute | solution.py:359
  27.5 14.8 %collective-permute-start.4 = (bf16[784,128]{1,0:T(8,128)(2,1)S(1)}, bf16[784,128]{1,0:T(8,128)(2,1)S(1)}, u32[]{:S(2)}, u32[]{:S(2)}) collective-permute-start(bf16[784,128]{1,0:T(8,128)(2,1)S(1)} %get-tuple-element.41), channel_id=1, source_target_pairs={{0,4},{1,5},{2,6},{3,7},{4,0},{5,1},{6,2},{7,3},{8,12},{9,13},{10,... | collective-permute-start | bytes 602120 | tf_op jit(solution)/shard_map/ppermute | solution.py:359
  29.0 34.6 %copy-start.17 = (s32[4,1]{0,1:T(1,128)S(1)}, s32[4,1]{0,1:T(1,128)}, u32[]{:S(2)}) copy-start(s32[4,1]{0,1:T(1,128)} %param.19) | copy-start | bytes 52
  29.0 34.6 %copy-start.18 = (s32[4,1]{0,1:T(1,128)S(1)}, s32[4,1]{0,1:T(1,128)}, u32[]{:S(2)}) copy-start(s32[4,1]{0,1:T(1,128)} %param.20) | copy-start | bytes 52
  29.1 34.7 %copy-start.11 = (s32[4,128]{1,0:T(4,128)S(1)}, s32[4,128]{1,0:T(4,128)}, u32[]{:S(2)}) copy-start(s32[4,128]{1,0:T(4,128)} %refs_4_.2) | copy-start | bytes 6148
  29.1 34.7 %copy-start.12 = (s32[4,128]{1,0:T(4,128)S(1)}, s32[4,128]{1,0:T(4,128)}, u32[]{:S(2)}) copy-start(s32[4,128]{1,0:T(4,128)} %refs_5_.3) | copy-start | bytes 6148
  31.2 12.5 %collective-permute-start.7 = (bf16[576,256]{1,0:T(8,128)(2,1)S(1)}, bf16[576,256]{1,0:T(8,128)(2,1)S(1)}, u32[]{:S(2)}, u32[]{:S(2)}) collective-permute-start(bf16[576,256]{1,0:T(8,128)(2,1)S(1)} %get-tuple-element.50), channel_id=1, source_target_pairs={{0,2},{1,3},{2,0},{3,1},{4,6},{5,7},{6,4},{7,5},{8,10},{9,11},{10,... | collective-permute-start | bytes 884744 | tf_op jit(solution)/shard_map/ppermute | solution.py:359
  31.2 11.0 %collective-permute-start.3 = (bf16[720,128]{1,0:T(8,128)(2,1)S(1)}, bf16[720,128]{1,0:T(8,128)(2,1)S(1)}, u32[]{:S(2)}, u32[]{:S(2)}) collective-permute-start(bf16[720,128]{1,0:T(8,128)(2,1)S(1)} %get-tuple-element.40), channel_id=1, source_target_pairs={{0,1},{1,0},{2,3},{3,2},{4,5},{5,4},{6,7},{7,6},{8,9},{9,8},{10,11... | collective-permute-start | bytes 552968 | tf_op jit(solution)/shard_map/ppermute | solution.py:359
  32.8 9.4 %collective-permute-start.5 = (bf16[720,128]{1,0:T(8,128)(2,1)S(1)}, bf16[720,128]{1,0:T(8,128)(2,1)S(1)}, u32[]{:S(2)}, u32[]{:S(2)}) collective-permute-start(bf16[720,128]{1,0:T(8,128)(2,1)S(1)} %get-tuple-element.42), channel_id=1, source_target_pairs={{0,5},{1,4},{2,7},{3,6},{4,1},{5,0},{6,3},{7,2},{8,13},{9,12},{10,... | collective-permute-start | bytes 552968 | tf_op jit(solution)/shard_map/ppermute | solution.py:359
  43.6 20.2 %collective-permute-start.6 = (bf16[784,256]{1,0:T(8,128)(2,1)S(1)}, bf16[784,256]{1,0:T(8,128)(2,1)S(1)}, u32[]{:S(2)}, u32[]{:S(2)}) collective-permute-start(bf16[784,256]{1,0:T(8,128)(2,1)S(1)} %get-tuple-element.45), channel_id=1, source_target_pairs={{0,2},{1,3},{2,0},{3,1},{4,6},{5,7},{6,4},{7,5},{8,10},{9,11},{10,... | collective-permute-start | bytes 1204232 | tf_op jit(solution)/shard_map/ppermute | solution.py:359
  44.8 39.0 %copy-start.4 = (f32[72,4]{1,0:T(8,128)S(1)}, f32[72,4]{1,0:T(8,128)}, u32[]{:S(2)}) copy-start(f32[72,4]{1,0:T(8,128)} %constant.16.clone.refs_8_) | copy-start | bytes 3460
  44.8 39.0 %copy-start.13 = (f32[1,1296]{1,0:T(1,128)S(1)}, f32[1,1296]{1,0:T(1,128)}, u32[]{:S(2)}) copy-start(f32[1,1296]{1,0:T(1,128)} %constant.17.clone.refs_9_) | copy-start | bytes 15556
  44.8 38.9 %copy-start.16 = (f32[36]{0:T(128)S(1)}, f32[36]{0:T(128)}, u32[]{:S(2)}) copy-start(f32[36]{0:T(128)} %constant.15.clone.group_ref) | copy-start | bytes 436
  44.8 6.3 %collective-permute-start.8 = (bf16[576,128]{1,0:T(8,128)(2,1)S(1)}, bf16[576,128]{1,0:T(8,128)(2,1)S(1)}, u32[]{:S(2)}, u32[]{:S(2)}) collective-permute-start(bf16[576,128]{1,0:T(8,128)(2,1)S(1)} %get-tuple-element.52), channel_id=1, source_target_pairs={{0,1},{1,0},{2,3},{3,2},{4,5},{5,4},{6,7},{7,6},{8,9},{9,8},{10,11... | collective-permute-start | bytes 442376 | tf_op jit(solution)/shard_map/ppermute | solution.py:359
  46.4 6.7 %collective-permute-start.9 = (bf16[576,128]{1,0:T(8,128)(2,1)S(1)}, bf16[576,128]{1,0:T(8,128)(2,1)S(1)}, u32[]{:S(2)}, u32[]{:S(2)}) collective-permute-start(bf16[576,128]{1,0:T(8,128)(2,1)S(1)} %get-tuple-element.53), channel_id=1, source_target_pairs={{0,4},{1,5},{2,6},{3,7},{4,0},{5,1},{6,2},{7,3},{8,12},{9,13},{10,... | collective-permute-start | bytes 442376 | tf_op jit(solution)/shard_map/ppermute | solution.py:359
  47.0 8.5 %collective-permute-start.10 = (bf16[576,128]{1,0:T(8,128)(2,1)S(1)}, bf16[576,128]{1,0:T(8,128)(2,1)S(1)}, u32[]{:S(2)}, u32[]{:S(2)}) collective-permute-start(bf16[576,128]{1,0:T(8,128)(2,1)S(1)} %get-tuple-element.54), channel_id=1, source_target_pairs={{0,5},{1,4},{2,7},{3,6},{4,1},{5,0},{6,3},{7,2},{8,13},{9,12},{10,... | collective-permute-start | bytes 442376 | tf_op jit(solution)/shard_map/ppermute | solution.py:359
  56.6 10.4 %collective-permute-start.11 = (bf16[576,128]{1,0:T(8,128)(2,1)S(1)}, bf16[576,128]{1,0:T(8,128)(2,1)S(1)}, u32[]{:S(2)}, u32[]{:S(2)}) collective-permute-start(bf16[576,128]{1,0:T(8,128)(2,1)S(1)} %get-tuple-element.56), channel_id=1, source_target_pairs={{0,8},{1,9},{2,10},{3,11},{4,12},{5,13},{6,14},{7,15},{8,16},{9,17... | collective-permute-start | bytes 442376 | tf_op jit(solution)/shard_map/ppermute | solution.py:359
  61.2 10.8 %collective-permute-start.12 = (bf16[576,128]{1,0:T(8,128)(2,1)S(1)}, bf16[576,128]{1,0:T(8,128)(2,1)S(1)}, u32[]{:S(2)}, u32[]{:S(2)}) collective-permute-start(bf16[576,128]{1,0:T(8,128)(2,1)S(1)} %get-tuple-element.57), channel_id=1, source_target_pairs={{0,16},{1,17},{2,18},{3,19},{4,20},{5,21},{6,22},{7,23},{8,24},{9,... | collective-permute-start | bytes 442376 | tf_op jit(solution)/shard_map/ppermute | solution.py:359
  62.8 9.2 %collective-permute-start.13 = (bf16[576,128]{1,0:T(8,128)(2,1)S(1)}, bf16[576,128]{1,0:T(8,128)(2,1)S(1)}, u32[]{:S(2)}, u32[]{:S(2)}) collective-permute-start(bf16[576,128]{1,0:T(8,128)(2,1)S(1)} %get-tuple-element.58), channel_id=1, source_target_pairs={{0,24},{1,25},{2,26},{3,27},{4,28},{5,29},{6,30},{7,31},{8,0},{9,1... | collective-permute-start | bytes 442376 | tf_op jit(solution)/shard_map/ppermute | solution.py:359
  74.0 9.7 %collective-permute-start.14 = (bf16[1304,128]{1,0:T(8,128)(2,1)S(1)}, bf16[1304,128]{1,0:T(8,128)(2,1)S(1)}, u32[]{:S(2)}, u32[]{:S(2)}) collective-permute-start(bf16[1304,128]{1,0:T(8,128)(2,1)S(1)} %get-tuple-element.61), channel_id=1, source_target_pairs={{0,1},{1,0},{2,3},{3,2},{4,5},{5,4},{6,7},{7,6},{8,9},{9,8},{10,11... | collective-permute-start | bytes 1001480 | tf_op jit(solution)/shard_map/ppermute | solution.py:698
  75.6 4.5 %collective-permute-start.15 = (bf16[4,1408]{1,0:T(4,128)(2,1)S(1)}, bf16[4,1408]{1,0:T(4,128)(2,1)S(1)}, u32[]{:S(2)}, u32[]{:S(2)}) collective-permute-start(bf16[4,1408]{1,0:T(4,128)(2,1)S(1)} %get-tuple-element.62), channel_id=1, source_target_pairs={{0,2},{2,0},{4,6},{6,4},{8,10},{10,8},{12,14},{14,12},{16,18},{18,... | collective-permute-start | bytes 33800 | tf_op jit(solution)/shard_map/ppermute | solution.py:700
  75.6 5.8 %collective-permute-start.16 = (bf16[4,1408]{1,0:T(4,128)(2,1)S(1)}, bf16[4,1408]{1,0:T(4,128)(2,1)S(1)}, u32[]{:S(2)}, u32[]{:S(2)}) collective-permute-start(bf16[4,1408]{1,0:T(4,128)(2,1)S(1)} %get-tuple-element.63), channel_id=1, source_target_pairs={{0,30},{2,4},{4,2},{6,8},{8,6},{10,12},{12,10},{14,16},{16,14},{18... | collective-permute-start | bytes 33800 | tf_op jit(solution)/shard_map/ppermute | solution.py:699
